TPU v7x, 512 devices: a whole 4x8x8 slice. The times are simulated.
512 devices in a mesh: gx: 16 (over z, x_lo), gy: 16 (over y, core), gz: 2 (over x_hi).
Axes of the slice: x: 4 (x_hi: 2, x_lo: 2; x = x_hi * 2 + x_lo), y: 8, z: 8, core: 2. Of those that a mesh axis runs over, the one named last changes fastest.
Arguments:
- tracers: float32 [5, 8, 2048, 2048], P(None, 'gz', 'gx', 'gy'), may hold values from 0 to 2
- wind_field: float32 [3, 8, 2048, 2048], P(None, 'gz', 'gx', 'gy'), may hold values from -0.2 to 0.2
- band_layer: int32 [2048, 2048], P('gx', 'gy'), may hold values from 0 to 6
- wall_mask: int32 [2048, 2048], P('gx', 'gy'), may hold values 0 or 1
- exit_mask: int32 [2048, 2048], P('gx', 'gy'), may hold values 0 or 1
- occupant_count: int32 [2048, 2048], P('gx', 'gy'), may hold values from 0 to 3
Outputs:
- tracers_out: float32 [5, 8, 2048, 2048], P(None, 'gz', 'gx', 'gy')
- occupants: float32 [2048, 2048], P('gx', 'gy')
- fed_density: float32 [2048, 2048], P('gx', 'gy')
All inputs are finite; a program needn't handle non-finite values. No bound on the sum of `wall_mask` or of `exit_mask` on one device may be relied on, other than what follows from the above.
Results may differ from a plain program's by a relative error of at most 0.00002.
Values sent between devices are 32-bit elements; how exact they have to be, the bound alone decides.
A program may use at most 64 MiB of HBM per device.

v0:
```python
import jax
import jax.numpy as jnp
from jax import lax
from jax.sharding import PartitionSpec as P

diffusivity = (0.05, 0.04, 0.06, 0.03, 0.045)


def extended(cells, sides, width):
    for axis, dim in sides:
        count = lax.axis_size(axis)
        ends = count - 1
        head = lax.slice_in_dim(cells, 0, width, axis=dim)
        tail = lax.slice_in_dim(cells, cells.shape[dim] - width, cells.shape[dim], axis=dim)
        cells = jnp.concatenate(
            [
                lax.ppermute(tail, axis, [(i, (i + 1) % count) for i in range(ends)]),
                cells,
                lax.ppermute(head, axis, [((i + 1) % count, i) for i in range(ends)]),
            ],
            axis=dim,
        )
    return cells


def passed_along(block, axis, distance):
    devices = range(lax.axis_size(axis))
    route = [(i - distance, i) for i in devices if i - distance in devices]
    return lax.ppermute(block, axis, route)


def advance(padded, wind):
    center = padded[:, 1:-1, 1:-1, 1:-1]
    z_lower = padded[:, :-2, 1:-1, 1:-1]
    z_upper = padded[:, 2:, 1:-1, 1:-1]
    x_lower = padded[:, 1:-1, :-2, 1:-1]
    x_upper = padded[:, 1:-1, 2:, 1:-1]
    y_lower = padded[:, 1:-1, 1:-1, :-2]
    y_upper = padded[:, 1:-1, 1:-1, 2:]
    laplace = x_lower + x_upper + y_lower + y_upper + z_lower + z_upper - 6.0 * center

    def upwind(velocity, lower, upper):
        return jnp.maximum(velocity, 0.0)[None] * (center - lower) + jnp.minimum(velocity, 0.0)[
            None
        ] * (upper - center)

    transport = (
        upwind(wind[0], x_lower, x_upper)
        + upwind(wind[1], y_lower, y_upper)
        + upwind(wind[2], z_lower, z_upper)
    )
    coefficient = jnp.array(diffusivity, jnp.float32)[:, None, None, None]
    return center + coefficient * laplace - transport


def toxic_rate(exposure):
    return (
        0.3 * exposure[0] * jnp.exp(0.3 * exposure[1])
        + 0.2 * exposure[2]
        + 0.1 * (2.0 - exposure[3]) ** 2
        + 0.1 * exposure[4] ** 2
    )


def crowd_step(occupants_pad, dose_pad, passable_pad, dose_rate, exit_share):
    occupants_mid = occupants_pad[1:-1, 1:-1]
    dose_mid = dose_pad[1:-1, 1:-1]
    gate_x = (
        0.25 * passable_pad[:-1, 1:-1] * passable_pad[1:, 1:-1] * (1.0 - occupants_pad[1:, 1:-1])
    )
    carry_x = gate_x * occupants_pad[:-1, 1:-1]
    dose_x = gate_x * dose_pad[:-1, 1:-1]
    gate_y = (
        0.15 * passable_pad[1:-1, :-1] * passable_pad[1:-1, 1:] * (1.0 - occupants_pad[1:-1, 1:])
    )
    carry_y = gate_y * occupants_pad[1:-1, :-1]
    dose_y = gate_y * dose_pad[1:-1, :-1]
    retain = 1.0 - 0.5 * exit_share
    occupants_new = (
        occupants_mid + carry_x[:-1] - carry_x[1:] + carry_y[:, :-1] - carry_y[:, 1:]
    ) * retain
    dose_new = (
        dose_mid
        + dose_x[:-1]
        - dose_x[1:]
        + dose_y[:, :-1]
        - dose_y[:, 1:]
        + dose_rate * occupants_mid
    ) * retain
    return (occupants_new, dose_new)


def on_device(tracers, wind_field, band_layer, wall_mask, exit_mask, occupant_count):
    layers_dev = tracers.shape[1]
    fields = tracers
    for step in range(2):
        padded = extended(fields, (("gx", 2), ("gy", 3), ("gz", 1)), 1)
        fields = advance(padded, wind_field)
    layers = (lax.axis_index("gz") * layers_dev + jnp.arange(layers_dev))[:, None, None]
    weight = ((layers == band_layer[None]) | (layers == band_layer[None] + 1)).astype(jnp.float32)
    partial_value = 0.5 * jnp.sum(fields * weight[None], axis=1)
    exposure = lax.psum(partial_value, "gz")
    dose_rate = toxic_rate(exposure)
    passable = 1.0 - wall_mask.astype(jnp.float32)
    exit_share = exit_mask.astype(jnp.float32)
    occupants = 0.25 * occupant_count.astype(jnp.float32) * passable
    dose = jnp.zeros_like(occupants)
    row_after = passed_along(passable[:1, :], "gx", -1)
    column_after = passed_along(passable[:, :1], "gy", -1)
    middle = jnp.concatenate([passable[:, :1], passable, column_after], axis=1)
    zero_cell = jnp.zeros((1, 1), jnp.float32)
    top_line = jnp.concatenate([zero_cell, passable[:1, :], zero_cell], axis=1)
    bottom_line = jnp.concatenate([zero_cell, row_after, zero_cell], axis=1)
    passable_pad = jnp.concatenate([top_line, middle, bottom_line], axis=0)
    for step in range(4):
        floor_pair = extended(jnp.stack([occupants, dose]), (("gx", 1), ("gy", 2)), 1)
        occupants, dose = crowd_step(
            floor_pair[0], floor_pair[1], passable_pad, dose_rate, exit_share
        )
    return (fields, occupants, dose)


def solution(mesh):
    return jax.shard_map(
        on_device,
        mesh=mesh,
        in_specs=(
            P(None, "gz", "gx", "gy"),
            P(None, "gz", "gx", "gy"),
            P("gx", "gy"),
            P("gx", "gy"),
            P("gx", "gy"),
            P("gx", "gy"),
        ),
        out_specs=(P(None, "gz", "gx", "gy"), P("gx", "gy"), P("gx", "gy")),
        check_vma=False,
    )
```

profile of v0, /device:TPU:155, one launch (start us, length us, event | category | flops | bytes accessed | tf_op | source)
XLA Modules:
  0.0 293.1 jit_solution(8191018380594196464)
XLA Ops:
  8.3 4.0 %collective-permute-start = (f32[5,4,1,128]{3,0,2,1:T(8,128)S(1)}, f32[5,4,1,128]{3,0,2,1:T(8,128)S(1)}, u32[]{:S(2)}, u32[]{:S(2)}) collective-permute-start(f32[5,4,1,128]{3,0,2,1:T(8,128)S(1)} %copy.232), channel_id=1, source_target_pairs={{0,32},{32,64},{64,96},{96,128},{128,160},{160,192},{192,224},{224... | collective-permute-start | bytes 30728 | tf_op jit(solution)/shard_map/ppermute | solution.py:17
  12.3 1.9 collective-permute-start.1
  15.7 4.2 %collective-permute-start.12 = (f32[2,1,128]{2,1,0:T(1,128)}, f32[2,1,128]{2,1,0:T(1,128)}, u32[]{:S(2)}, u32[]{:S(2)}) collective-permute-start(f32[2,1,128]{2,1,0:T(1,128)} %get-tuple-element.90), channel_id=1, source_target_pairs={{0,32},{32,64},{64,96},{96,128},{128,160},{160,192},{192,224},{224... | collective-permute-start | bytes 3080 | tf_op jit(solution)/shard_map/ppermute | solution.py:17
  20.0 1.9 collective-permute-start.13
  21.9 3.4 %collective-permute-start.16 = (f32[128,1]{1,0:T(8,128)S(1)}, f32[128,1]{1,0:T(8,128)}, u32[]{:S(2)}, u32[]{:S(2)}) collective-permute-start(f32[128,1]{1,0:T(8,128)S(1)} %bitcast.46), channel_id=1, source_target_pairs={{2,0},{4,2},{6,4},{8,6},{10,8},{12,10},{14,12},{16,14},{18,16},{20... | collective-permute-start | bytes 1544 | tf_op jit(solution)/shard_map/ppermute | solution.py:29
  25.3 2.1 maximum_bitcast_fusion.2
  27.4 1.8 copy.205
  30.1 2.0 copy.196
  32.2 1.5 pad_maximum_fusion.67
  33.6 4.3 %collective-permute-start.2 = (f32[5,4,130,1]{2,0,3,1:T(8,128)}, f32[5,4,130,1]{2,0,3,1:T(8,128)}, u32[]{:S(2)}, u32[]{:S(2)}) collective-permute-start(f32[5,4,130,1]{2,0,3,1:T(8,128)} %get-tuple-element.35), channel_id=1, source_target_pairs={{0,2},{2,4},{4,6},{6,8},{8,10},{10,12},{12,14},{14,16},{16,18},{18... | collective-permute-start | bytes 31208 | tf_op jit(solution)/shard_map/ppermute | solution.py:17
  38.0 1.9 collective-permute-start.3
  42.4 1.9 copy.208
  48.3 2.7 collective-permute-start.17
  51.0 3.4 %pad_maximum_fusion.45 = (f32[5,1,130,130]{2,0,3,1:T(8,128)}, f32[5,1,130,130]{2,0,3,1:T(8,128)S(1)}) fusion(f32[5,4,130,1]{2,0,3,1:T(8,128)} %collective-permute-done.3, f32[5,4,130,1]{2,0,3,1:T(8,128)} %collective-permute-done.2, f32[5,4,1,128]{2,0,3,1:T(8,128)} %copy.196, f32[5,4,128,128]{2,0,3,1:T(8,128)} %copy.205, f32[5,4,1,128]{2,0,3,1:T(8,128)S(1)} %copy.192), kind=kLoop, calls=%fused_computation.48 | loop fusion | flops 676000 | bytes 2028000 | tf_op jit(solution)/shard_map/slice | solution.py:14
  54.5 2.6 copy.200
  57.0 4.1 %collective-permute-start.4 = (f32[5,1,130,130]{3,2,1,0:T(8,128)}, f32[5,1,130,130]{3,2,1,0:T(8,128)S(1)}, u32[]{:S(2)}, u32[]{:S(2)}) collective-permute-start(f32[5,1,130,130]{3,2,1,0:T(8,128)} %copy.200), channel_id=1, source_target_pairs={{0,1},{2,3},{4,5},{6,7},{8,9},{10,11},{12,13},{14,15},{16,17},{18,... | collective-permute-start | bytes 1014008 | tf_op jit(solution)/shard_map/ppermute | solution.py:17
  61.6 1.3 collective-permute-start.5
  64.3 5.4 %collective-permute-start.14 = (f32[2,130,1]{2,1,0:T(8,128)}, f32[2,130,1]{2,1,0:T(8,128)}, u32[]{:S(2)}, u32[]{:S(2)}) collective-permute-start(f32[2,130,1]{2,1,0:T(8,128)} %get-tuple-element.80), channel_id=1, source_target_pairs={{0,2},{2,4},{4,6},{6,8},{8,10},{10,12},{12,14},{14,16},{16,18},{18... | collective-permute-start | bytes 3128 | tf_op jit(solution)/shard_map/ppermute | solution.py:17
  69.7 7.0 %collective-permute-done.4 = f32[5,1,130,130]{3,2,1,0:T(8,128)S(1)} collective-permute-done((f32[5,1,130,130]{3,2,1,0:T(8,128)}, f32[5,1,130,130]{3,2,1,0:T(8,128)S(1)}, u32[]{:S(2)}, u32[]{:S(2)}) %collective-permute-start.4) | collective-permute-done | bytes 338032 | tf_op jit(solution)/shard_map/ppermute | solution.py:17
  76.7 2.4 collective-permute-start.15
  79.8 2.6 collective-permute-done.5
  82.4 2.7 copy.203
  85.2 13.5 %add_subtract_fusion.1 = f32[5,4,128,128]{2,0,3,1:T(8,128)S(1)} fusion(f32[5,4,128,128]{2,0,3,1:T(8,128)} %copy.205, f32[5,1,130,130]{2,0,3,1:T(8,128)} %copy.203, f32[5,4,130,1]{2,0,3,1:T(8,128)} %collective-permute-done.3, f32[5,4,1,128]{2,0,3,1:T(8,128)} %copy.196, f32[5,4,1,128]{2,0,3,1:T(8,128)} %copy-done.2, ...), kind=kLoop, calls=%fused_computation.38 | loop fusion | flops 14745600 | bytes 4911604 | tf_op jit(solution)/shard_map/sub | solution.py:53
  98.7 2.6 fusion.43
  101.3 2.2 copy.218
  103.6 4.5 %collective-permute-start.6 = (f32[5,4,1,128]{3,0,2,1:T(8,128)S(1)}, f32[5,4,1,128]{3,0,2,1:T(8,128)S(1)}, u32[]{:S(2)}, u32[]{:S(2)}) collective-permute-start(f32[5,4,1,128]{3,0,2,1:T(8,128)S(1)} %copy.218), channel_id=1, source_target_pairs={{0,32},{32,64},{64,96},{96,128},{128,160},{160,192},{192,224},{224... | collective-permute-start | bytes 30728 | tf_op jit(solution)/shard_map/ppermute | solution.py:17
  108.1 2.2 copy.220
  110.3 1.9 collective-permute-start.7
  113.4 2.0 copy.219
  115.8 2.0 copy.221
  118.8 4.3 %collective-permute-start.8 = (f32[5,4,130,1]{2,0,3,1:T(8,128)S(1)}, f32[5,4,130,1]{2,0,3,1:T(8,128)S(1)}, u32[]{:S(2)}, u32[]{:S(2)}) collective-permute-start(f32[5,4,130,1]{2,0,3,1:T(8,128)S(1)} %get-tuple-element.33), channel_id=1, source_target_pairs={{0,2},{2,4},{4,6},{6,8},{8,10},{10,12},{12,14},{14,16},{16,18},{18... | collective-permute-start | bytes 31208 | tf_op jit(solution)/shard_map/ppermute | solution.py:17
  123.1 2.1 collective-permute-start.9
  125.9 3.7 %collective-permute-done.9 = f32[5,4,130,1]{2,0,3,1:T(8,128)S(1)} collective-permute-done((f32[5,4,130,1]{2,0,3,1:T(8,128)S(1)}, f32[5,4,130,1]{2,0,3,1:T(8,128)S(1)}, u32[]{:S(2)}, u32[]{:S(2)}) %collective-permute-start.9) | collective-permute-done | bytes 10432 | tf_op jit(solution)/shard_map/ppermute | solution.py:19
  130.2 1.9 pad_maximum_fusion.40
  132.0 2.5 copy.224
  134.5 4.6 %collective-permute-start.10 = (f32[5,1,130,130]{3,2,1,0:T(8,128)}, f32[5,1,130,130]{3,2,1,0:T(8,128)}, u32[]{:S(2)}, u32[]{:S(2)}) collective-permute-start(f32[5,1,130,130]{3,2,1,0:T(8,128)} %copy.224), channel_id=1, source_target_pairs={{0,1},{2,3},{4,5},{6,7},{8,9},{10,11},{12,13},{14,15},{16,17},{18,... | collective-permute-start | bytes 1014008 | tf_op jit(solution)/shard_map/ppermute | solution.py:17
  139.1 1.3 copy.226
  141.7 1.4 slice_multiply_fusion.15
  143.2 1.8 slice_multiply_fusion.7
  145.0 6.2 %collective-permute-done.10 = f32[5,1,130,130]{3,2,1,0:T(8,128)} collective-permute-done((f32[5,1,130,130]{3,2,1,0:T(8,128)}, f32[5,1,130,130]{3,2,1,0:T(8,128)}, u32[]{:S(2)}, u32[]{:S(2)}) %collective-permute-start.10) | collective-permute-done | bytes 338032 | tf_op jit(solution)/shard_map/ppermute | solution.py:17
  151.1 1.8 copy.225
  153.0 5.9 %collective-permute-done.11 = f32[5,1,130,130]{3,2,1,0:T(8,128)} collective-permute-done((f32[5,1,130,130]{3,2,1,0:T(8,128)}, f32[5,1,130,130]{3,2,1,0:T(8,128)}, u32[]{:S(2)}, u32[]{:S(2)}) %collective-permute-start.11) | collective-permute-done | bytes 338032 | tf_op jit(solution)/shard_map/ppermute | solution.py:19
  158.9 2.7 copy.227
  161.6 11.6 %multiply_reduce_fusion = (f32[5,128,128]{1,0,2:T(8,128)}, f32[5,4,128,128]{2,0,3,1:T(8,128)}) fusion(f32[4,128,128]{1,2,0:T(8,128)} %or_convert_fusion, f32[5,4,128,128]{2,0,3,1:T(8,128)S(1)} %add_subtract_fusion.1, f32[4,128,128]{1,2,0:T(8,128)} %copy.216, f32[4,128,128]{1,2,0:T(8,128)} %copy.214, f32[4,128,128]{1,2,0:T(8,128)} %copy.212, ...), kind=kLoop, calls=%fused_computation.36 | loop fusion | flops 15319040 | bytes 5501428 | tf_op jit(solution)/shard_map/reduce_sum | solution.py:101
  176.4 42.5 %all-reduce.3.cloned.1.call-done = f32[5,128,128]{2,1,0:T(8,128)} async-done(((f32[5,128,128]{2,1,0:T(8,128)}), f32[5,128,128]{2,1,0:T(8,128)}) %all-reduce.3.cloned.1.call-update) | async-done | bytes 327696 | tf_op jit(solution)/shard_map/psum | solution.py:102
  220.0 4.2 %collective-permute-start.18 = (f32[2,1,128]{2,1,0:T(1,128)S(1)}, f32[2,1,128]{2,1,0:T(1,128)S(1)}, u32[]{:S(2)}, u32[]{:S(2)}) collective-permute-start(f32[2,1,128]{2,1,0:T(1,128)S(1)} %get-tuple-element.86), channel_id=1, source_target_pairs={{0,32},{32,64},{64,96},{96,128},{128,160},{160,192},{192,224},{224... | collective-permute-start | bytes 3080 | tf_op jit(solution)/shard_map/ppermute | solution.py:17
  224.2 1.9 collective-permute-start.19
  226.1 3.3 %collective-permute-done.19 = f32[2,1,128]{2,1,0:T(1,128)S(1)} collective-permute-done((f32[2,1,128]{2,1,0:T(1,128)S(1)}, f32[2,1,128]{2,1,0:T(1,128)S(1)}, u32[]{:S(2)}, u32[]{:S(2)}) %collective-permute-start.19) | collective-permute-done | bytes 1056 | tf_op jit(solution)/shard_map/ppermute | solution.py:19
  229.5 6.3 %collective-permute-start.20 = (f32[2,130,1]{2,1,0:T(8,128)S(1)}, f32[2,130,1]{2,1,0:T(8,128)S(1)}, u32[]{:S(2)}, u32[]{:S(2)}) collective-permute-start(f32[2,130,1]{2,1,0:T(8,128)S(1)} %get-tuple-element.78), channel_id=1, source_target_pairs={{0,2},{2,4},{4,6},{6,8},{8,10},{10,12},{12,14},{14,16},{16,18},{18... | collective-permute-start | bytes 3128 | tf_op jit(solution)/shard_map/ppermute | solution.py:17
  235.9 1.9 collective-permute-start.21
  237.9 5.6 %collective-permute-done.21 = f32[2,130,1]{2,1,0:T(8,128)S(1)} collective-permute-done((f32[2,130,1]{2,1,0:T(8,128)S(1)}, f32[2,130,1]{2,1,0:T(8,128)S(1)}, u32[]{:S(2)}, u32[]{:S(2)}) %collective-permute-start.21) | collective-permute-done | bytes 1072 | tf_op jit(solution)/shard_map/ppermute | solution.py:19
  244.1 3.0 %collective-permute-start.22 = (f32[2,1,128]{2,1,0:T(1,128)S(1)}, f32[2,1,128]{2,1,0:T(1,128)S(1)}, u32[]{:S(2)}, u32[]{:S(2)}) collective-permute-start(f32[2,1,128]{2,1,0:T(1,128)S(1)} %get-tuple-element.84), channel_id=1, source_target_pairs={{0,32},{32,64},{64,96},{96,128},{128,160},{160,192},{192,224},{224... | collective-permute-start | bytes 3080 | tf_op jit(solution)/shard_map/ppermute | solution.py:17
  247.2 2.2 collective-permute-start.23
  249.4 4.4 %collective-permute-done.23 = f32[2,1,128]{2,1,0:T(1,128)S(1)} collective-permute-done((f32[2,1,128]{2,1,0:T(1,128)S(1)}, f32[2,1,128]{2,1,0:T(1,128)S(1)}, u32[]{:S(2)}, u32[]{:S(2)}) %collective-permute-start.23) | collective-permute-done | bytes 1056 | tf_op jit(solution)/shard_map/ppermute | solution.py:19
  254.0 2.9 collective-permute-start.24
  256.9 2.1 collective-permute-start.25
  259.0 5.6 %collective-permute-done.25 = f32[2,130,1]{2,1,0:T(8,128)S(1)} collective-permute-done((f32[2,130,1]{2,1,0:T(8,128)S(1)}, f32[2,130,1]{2,1,0:T(8,128)S(1)}, u32[]{:S(2)}, u32[]{:S(2)}) %collective-permute-start.25) | collective-permute-done | bytes 1072 | tf_op jit(solution)/shard_map/ppermute | solution.py:19
  265.3 3.6 %collective-permute-start.26 = (f32[2,1,128]{2,1,0:T(1,128)S(1)}, f32[2,1,128]{2,1,0:T(1,128)S(1)}, u32[]{:S(2)}, u32[]{:S(2)}) collective-permute-start(f32[2,1,128]{2,1,0:T(1,128)S(1)} %get-tuple-element.82), channel_id=1, source_target_pairs={{0,32},{32,64},{64,96},{96,128},{128,160},{160,192},{192,224},{224... | collective-permute-start | bytes 3080 | tf_op jit(solution)/shard_map/ppermute | solution.py:17
  268.9 1.9 collective-permute-start.27
  270.9 3.3 %collective-permute-done.27 = f32[2,1,128]{2,1,0:T(1,128)S(1)} collective-permute-done((f32[2,1,128]{2,1,0:T(1,128)S(1)}, f32[2,1,128]{2,1,0:T(1,128)S(1)}, u32[]{:S(2)}, u32[]{:S(2)}) %collective-permute-start.27) | collective-permute-done | bytes 1056 | tf_op jit(solution)/shard_map/ppermute | solution.py:19
  274.3 3.2 %collective-permute-start.28 = (f32[2,130,1]{2,1,0:T(8,128)S(1)}, f32[2,130,1]{2,1,0:T(8,128)S(1)}, u32[]{:S(2)}, u32[]{:S(2)}) collective-permute-start(f32[2,130,1]{2,1,0:T(8,128)S(1)} %get-tuple-element.74), channel_id=1, source_target_pairs={{0,2},{2,4},{4,6},{6,8},{8,10},{10,12},{12,14},{14,16},{16,18},{18... | collective-permute-start | bytes 3128 | tf_op jit(solution)/shard_map/ppermute | solution.py:17
  277.5 1.9 collective-permute-start.29
  279.4 1.5 copy.231
  280.9 4.2 %collective-permute-done.29 = f32[2,130,1]{2,1,0:T(8,128)S(1)} collective-permute-done((f32[2,130,1]{2,1,0:T(8,128)S(1)}, f32[2,130,1]{2,1,0:T(8,128)S(1)}, u32[]{:S(2)}, u32[]{:S(2)}) %collective-permute-start.29) | collective-permute-done | bytes 1072 | tf_op jit(solution)/shard_map/ppermute | solution.py:19
  (110 shorter events, 24.8 us)
Async XLA Ops:
  7.2 20.3 %copy-start.7 = (f32[5,4,128,128]{3,2,1,0:T(8,128)S(1)}, f32[5,4,128,128]{3,2,1,0:T(8,128)}, u32[]{:S(2)}) copy-start(f32[5,4,128,128]{3,2,1,0:T(8,128)} %param.8) | copy-start | bytes 3932164
  7.2 20.2 %copy-start.14 = (s32[128,128]{1,0:T(8,128)S(1)}, s32[128,128]{1,0:T(8,128)}, u32[]{:S(2)}) copy-start(s32[128,128]{1,0:T(8,128)} %param.10) | copy-start | bytes 196612
  7.2 211.7 %all-reduce.3.cloned.1.call-start = ((), (), s32[]{:S(2)}) async-start(), calls=%async_computation | async-start | bytes 655360 | tf_op jit(solution)/shard_map/psum | solution.py:102
  8.3 21.1 %collective-permute-start = (f32[5,4,1,128]{3,0,2,1:T(8,128)S(1)}, f32[5,4,1,128]{3,0,2,1:T(8,128)S(1)}, u32[]{:S(2)}, u32[]{:S(2)}) collective-permute-start(f32[5,4,1,128]{3,0,2,1:T(8,128)S(1)} %copy.232), channel_id=1, source_target_pairs={{0,32},{32,64},{64,96},{96,128},{128,160},{160,192},{192,224},{224... | collective-permute-start | bytes 30728 | tf_op jit(solution)/shard_map/ppermute | solution.py:17
  12.3 17.9 %collective-permute-start.1 = (f32[5,4,1,128]{3,0,2,1:T(8,128)S(1)}, f32[5,4,1,128]{3,0,2,1:T(8,128)S(1)}, u32[]{:S(2)}, u32[]{:S(2)}) collective-permute-start(f32[5,4,1,128]{3,0,2,1:T(8,128)S(1)} %copy.233), channel_id=1, source_target_pairs={{32,0},{64,32},{96,64},{128,96},{160,128},{192,160},{224,192},{256... | collective-permute-start | bytes 30728 | tf_op jit(solution)/shard_map/ppermute | solution.py:19
  15.1 25.6 %copy-start.5 = (f32[128,128]{1,0:T(8,128)}, f32[128,128]{1,0:T(8,128)S(1)}, u32[]{:S(2)}) copy-start(f32[128,128]{1,0:T(8,128)S(1)} %get-tuple-element.88) | copy-start | bytes 196612
  15.7 45.8 %collective-permute-start.12 = (f32[2,1,128]{2,1,0:T(1,128)}, f32[2,1,128]{2,1,0:T(1,128)}, u32[]{:S(2)}, u32[]{:S(2)}) collective-permute-start(f32[2,1,128]{2,1,0:T(1,128)} %get-tuple-element.90), channel_id=1, source_target_pairs={{0,32},{32,64},{64,96},{96,128},{128,160},{160,192},{192,224},{224... | collective-permute-start | bytes 3080 | tf_op jit(solution)/shard_map/ppermute | solution.py:17
  20.0 42.9 %collective-permute-start.13 = (f32[2,1,128]{2,1,0:T(1,128)}, f32[2,1,128]{2,1,0:T(1,128)}, u32[]{:S(2)}, u32[]{:S(2)}) collective-permute-start(f32[2,1,128]{2,1,0:T(1,128)} %get-tuple-element.91), channel_id=1, source_target_pairs={{32,0},{64,32},{96,64},{128,96},{160,128},{192,160},{224,192},{256... | collective-permute-start | bytes 3080 | tf_op jit(solution)/shard_map/ppermute | solution.py:19
  21.9 119.8 %collective-permute-start.16 = (f32[128,1]{1,0:T(8,128)S(1)}, f32[128,1]{1,0:T(8,128)}, u32[]{:S(2)}, u32[]{:S(2)}) collective-permute-start(f32[128,1]{1,0:T(8,128)S(1)} %bitcast.46), channel_id=1, source_target_pairs={{2,0},{4,2},{6,4},{8,6},{10,8},{12,10},{14,12},{16,14},{18,16},{20... | collective-permute-start | bytes 1544 | tf_op jit(solution)/shard_map/ppermute | solution.py:29
  30.1 20.9 %copy-start.2 = (f32[5,4,1,128]{2,0,3,1:T(8,128)}, f32[5,4,1,128]{2,0,3,1:T(8,128)S(1)}, u32[]{:S(2)}) copy-start(f32[5,4,1,128]{2,0,3,1:T(8,128)S(1)} %copy.192) | copy-start | bytes 30724
  33.6 14.7 %collective-permute-start.2 = (f32[5,4,130,1]{2,0,3,1:T(8,128)}, f32[5,4,130,1]{2,0,3,1:T(8,128)}, u32[]{:S(2)}, u32[]{:S(2)}) collective-permute-start(f32[5,4,130,1]{2,0,3,1:T(8,128)} %get-tuple-element.35), channel_id=1, source_target_pairs={{0,2},{2,4},{4,6},{6,8},{8,10},{10,12},{12,14},{14,16},{16,18},{18... | collective-permute-start | bytes 31208 | tf_op jit(solution)/shard_map/ppermute | solution.py:17
  38.0 13.1 %collective-permute-start.3 = (f32[5,4,130,1]{2,0,3,1:T(8,128)}, f32[5,4,130,1]{2,0,3,1:T(8,128)}, u32[]{:S(2)}, u32[]{:S(2)}) collective-permute-start(f32[5,4,130,1]{2,0,3,1:T(8,128)} %get-tuple-element.36), channel_id=1, source_target_pairs={{2,0},{4,2},{6,4},{8,6},{10,8},{12,10},{14,12},{16,14},{18,16},{20... | collective-permute-start | bytes 31208 | tf_op jit(solution)/shard_map/ppermute | solution.py:19
  42.4 42.8 %copy-start.4 = (f32[4,128,128]{1,2,0:T(8,128)}, f32[4,128,128]{1,2,0:T(8,128)S(1)}, u32[]{:S(2)}) copy-start(f32[4,128,128]{1,2,0:T(8,128)S(1)} %copy.206) | copy-start | bytes 786436
  48.3 93.4 %collective-permute-start.17 = (f32[1,128]{1,0:T(1,128)}, f32[1,128]{1,0:T(1,128)S(1)}, u32[]{:S(2)}, u32[]{:S(2)}) collective-permute-start(f32[1,128]{1,0:T(1,128)} %slice.537), channel_id=1, source_target_pairs={{32,0},{64,32},{96,64},{128,96},{160,128},{192,160},{224,192},{256... | collective-permute-start | bytes 1544 | tf_op jit(solution)/shard_map/ppermute | solution.py:29
  54.5 8.4 %copy-start.9 = (f32[2,128,128]{2,1,0:T(8,128)S(1)}, f32[2,128,128]{2,1,0:T(8,128)}, u32[]{:S(2)}) copy-start(f32[2,128,128]{2,1,0:T(8,128)} %stack.34) | copy-start | bytes 393220
  57.0 19.7 %collective-permute-start.4 = (f32[5,1,130,130]{3,2,1,0:T(8,128)}, f32[5,1,130,130]{3,2,1,0:T(8,128)S(1)}, u32[]{:S(2)}, u32[]{:S(2)}) collective-permute-start(f32[5,1,130,130]{3,2,1,0:T(8,128)} %copy.200), channel_id=1, source_target_pairs={{0,1},{2,3},{4,5},{6,7},{8,9},{10,11},{12,13},{14,15},{16,17},{18,... | collective-permute-start | bytes 1014008 | tf_op jit(solution)/shard_map/ppermute | solution.py:17
  61.6 20.9 %collective-permute-start.5 = (f32[5,1,130,130]{3,2,1,0:T(8,128)S(1)}, f32[5,1,130,130]{3,2,1,0:T(8,128)}, u32[]{:S(2)}, u32[]{:S(2)}) collective-permute-start(f32[5,1,130,130]{3,2,1,0:T(8,128)S(1)} %copy.202), channel_id=1, source_target_pairs={{1,0},{3,2},{5,4},{7,6},{9,8},{11,10},{13,12},{15,14},{17,16},{19,... | collective-permute-start | bytes 1014008 | tf_op jit(solution)/shard_map/ppermute | solution.py:19
  63.5 21.6 %copy-start.16 = (f32[5]{0:T(128)S(1)}, f32[5]{0:T(128)}, u32[]{:S(2)}) copy-start(f32[5]{0:T(128)} %constant.9.clone) | copy-start | bytes 64
  64.3 46.0 %collective-permute-start.14 = (f32[2,130,1]{2,1,0:T(8,128)}, f32[2,130,1]{2,1,0:T(8,128)}, u32[]{:S(2)}, u32[]{:S(2)}) collective-permute-start(f32[2,130,1]{2,1,0:T(8,128)} %get-tuple-element.80), channel_id=1, source_target_pairs={{0,2},{2,4},{4,6},{6,8},{8,10},{10,12},{12,14},{14,16},{16,18},{18... | collective-permute-start | bytes 3128 | tf_op jit(solution)/shard_map/ppermute | solution.py:17
  76.7 35.5 %collective-permute-start.15 = (f32[2,130,1]{2,1,0:T(8,128)}, f32[2,130,1]{2,1,0:T(8,128)}, u32[]{:S(2)}, u32[]{:S(2)}) collective-permute-start(f32[2,130,1]{2,1,0:T(8,128)} %get-tuple-element.81), channel_id=1, source_target_pairs={{2,0},{4,2},{6,4},{8,6},{10,8},{12,10},{14,12},{16,14},{18,16},{20... | collective-permute-start | bytes 3128 | tf_op jit(solution)/shard_map/ppermute | solution.py:19
  101.3 10.9 %copy-start.10 = (f32[2,128,128]{2,1,0:T(8,128)S(1)}, f32[2,128,128]{2,1,0:T(8,128)}, u32[]{:S(2)}) copy-start(f32[2,128,128]{2,1,0:T(8,128)} %stack.34) | copy-start | bytes 393220
  103.6 9.9 %collective-permute-start.6 = (f32[5,4,1,128]{3,0,2,1:T(8,128)S(1)}, f32[5,4,1,128]{3,0,2,1:T(8,128)S(1)}, u32[]{:S(2)}, u32[]{:S(2)}) collective-permute-start(f32[5,4,1,128]{3,0,2,1:T(8,128)S(1)} %copy.218), channel_id=1, source_target_pairs={{0,32},{32,64},{64,96},{96,128},{128,160},{160,192},{192,224},{224... | collective-permute-start | bytes 30728 | tf_op jit(solution)/shard_map/ppermute | solution.py:17
  110.3 5.5 %collective-permute-start.7 = (f32[5,4,1,128]{3,0,2,1:T(8,128)S(1)}, f32[5,4,1,128]{3,0,2,1:T(8,128)S(1)}, u32[]{:S(2)}, u32[]{:S(2)}) collective-permute-start(f32[5,4,1,128]{3,0,2,1:T(8,128)S(1)} %copy.220), channel_id=1, source_target_pairs={{32,0},{64,32},{96,64},{128,96},{160,128},{192,160},{224,192},{256... | collective-permute-start | bytes 30728 | tf_op jit(solution)/shard_map/ppermute | solution.py:19
  117.8 12.4 %copy-start = (f32[5,4,1,128]{2,0,3,1:T(8,128)S(1)}, f32[5,4,1,128]{2,0,3,1:T(8,128)}, u32[]{:S(2)}) copy-start(f32[5,4,1,128]{2,0,3,1:T(8,128)} %copy.219) | copy-start | bytes 30724
  117.8 12.4 %copy-start.1 = (f32[5,4,1,128]{2,0,3,1:T(8,128)S(1)}, f32[5,4,1,128]{2,0,3,1:T(8,128)}, u32[]{:S(2)}) copy-start(f32[5,4,1,128]{2,0,3,1:T(8,128)} %copy.221) | copy-start | bytes 30724
  118.8 7.1 %collective-permute-start.8 = (f32[5,4,130,1]{2,0,3,1:T(8,128)S(1)}, f32[5,4,130,1]{2,0,3,1:T(8,128)S(1)}, u32[]{:S(2)}, u32[]{:S(2)}) collective-permute-start(f32[5,4,130,1]{2,0,3,1:T(8,128)S(1)} %get-tuple-element.33), channel_id=1, source_target_pairs={{0,2},{2,4},{4,6},{6,8},{8,10},{10,12},{12,14},{14,16},{16,18},{18... | collective-permute-start | bytes 31208 | tf_op jit(solution)/shard_map/ppermute | solution.py:17
  123.1 6.4 %collective-permute-start.9 = (f32[5,4,130,1]{2,0,3,1:T(8,128)S(1)}, f32[5,4,130,1]{2,0,3,1:T(8,128)S(1)}, u32[]{:S(2)}, u32[]{:S(2)}) collective-permute-start(f32[5,4,130,1]{2,0,3,1:T(8,128)S(1)} %get-tuple-element.34), channel_id=1, source_target_pairs={{2,0},{4,2},{6,4},{8,6},{10,8},{12,10},{14,12},{16,14},{18,16},{20... | collective-permute-start | bytes 31208 | tf_op jit(solution)/shard_map/ppermute | solution.py:19
  129.6 0.6 copy-start.15
  132.0 9.7 %copy-start.6 = (f32[128,128]{1,0:T(8,128)S(1)}, f32[128,128]{1,0:T(8,128)}, u32[]{:S(2)}) copy-start(f32[128,128]{1,0:T(8,128)} %copy-done.5) | copy-start | bytes 196612
  134.5 16.6 %collective-permute-start.10 = (f32[5,1,130,130]{3,2,1,0:T(8,128)}, f32[5,1,130,130]{3,2,1,0:T(8,128)}, u32[]{:S(2)}, u32[]{:S(2)}) collective-permute-start(f32[5,1,130,130]{3,2,1,0:T(8,128)} %copy.224), channel_id=1, source_target_pairs={{0,1},{2,3},{4,5},{6,7},{8,9},{10,11},{12,13},{14,15},{16,17},{18,... | collective-permute-start | bytes 1014008 | tf_op jit(solution)/shard_map/ppermute | solution.py:17
  140.4 18.4 %collective-permute-start.11 = (f32[5,1,130,130]{3,2,1,0:T(8,128)}, f32[5,1,130,130]{3,2,1,0:T(8,128)}, u32[]{:S(2)}, u32[]{:S(2)}) collective-permute-start(f32[5,1,130,130]{3,2,1,0:T(8,128)} %copy.226), channel_id=1, source_target_pairs={{1,0},{3,2},{5,4},{7,6},{9,8},{11,10},{13,12},{15,14},{17,16},{19,... | collective-permute-start | bytes 1014008 | tf_op jit(solution)/shard_map/ppermute | solution.py:19
  173.2 3.1 %copy-start.8 = (f32[130,130]{1,0:T(8,128)S(1)}, f32[130,130]{1,0:T(8,128)}, u32[]{:S(2)}) copy-start(f32[130,130]{1,0:T(8,128)} %get-tuple-element.54) | copy-start | bytes 202804
  173.2 45.7 %copy-start.11 = (s32[128,128]{1,0:T(8,128)S(1)}, s32[128,128]{1,0:T(8,128)}, u32[]{:S(2)}) copy-start(s32[128,128]{1,0:T(8,128)} %param.12) | copy-start | bytes 196612
  173.2 45.7 %copy-start.12 = (f32[129,128]{1,0:T(8,128)S(1)}, f32[129,128]{1,0:T(8,128)}, u32[]{:S(2)}) copy-start(f32[129,128]{1,0:T(8,128)} %get-tuple-element.21) | copy-start | bytes 198148
  173.2 45.7 %copy-start.13 = (f32[128,129]{1,0:T(8,128)S(1)}, f32[128,129]{1,0:T(8,128)}, u32[]{:S(2)}) copy-start(f32[128,129]{1,0:T(8,128)} %get-tuple-element.23) | copy-start | bytes 198148
  220.0 6.1 %collective-permute-start.18 = (f32[2,1,128]{2,1,0:T(1,128)S(1)}, f32[2,1,128]{2,1,0:T(1,128)S(1)}, u32[]{:S(2)}, u32[]{:S(2)}) collective-permute-start(f32[2,1,128]{2,1,0:T(1,128)S(1)} %get-tuple-element.86), channel_id=1, source_target_pairs={{0,32},{32,64},{64,96},{96,128},{128,160},{160,192},{192,224},{224... | collective-permute-start | bytes 3080 | tf_op jit(solution)/shard_map/ppermute | solution.py:17
  224.2 5.2 %collective-permute-start.19 = (f32[2,1,128]{2,1,0:T(1,128)S(1)}, f32[2,1,128]{2,1,0:T(1,128)S(1)}, u32[]{:S(2)}, u32[]{:S(2)}) collective-permute-start(f32[2,1,128]{2,1,0:T(1,128)S(1)} %get-tuple-element.87), channel_id=1, source_target_pairs={{32,0},{64,32},{96,64},{128,96},{160,128},{192,160},{224,192},{256... | collective-permute-start | bytes 3080 | tf_op jit(solution)/shard_map/ppermute | solution.py:19
  229.5 8.4 %collective-permute-start.20 = (f32[2,130,1]{2,1,0:T(8,128)S(1)}, f32[2,130,1]{2,1,0:T(8,128)S(1)}, u32[]{:S(2)}, u32[]{:S(2)}) collective-permute-start(f32[2,130,1]{2,1,0:T(8,128)S(1)} %get-tuple-element.78), channel_id=1, source_target_pairs={{0,2},{2,4},{4,6},{6,8},{8,10},{10,12},{12,14},{14,16},{16,18},{18... | collective-permute-start | bytes 3128 | tf_op jit(solution)/shard_map/ppermute | solution.py:17
  235.9 7.6 %collective-permute-start.21 = (f32[2,130,1]{2,1,0:T(8,128)S(1)}, f32[2,130,1]{2,1,0:T(8,128)S(1)}, u32[]{:S(2)}, u32[]{:S(2)}) collective-permute-start(f32[2,130,1]{2,1,0:T(8,128)S(1)} %get-tuple-element.79), channel_id=1, source_target_pairs={{2,0},{4,2},{6,4},{8,6},{10,8},{12,10},{14,12},{16,14},{18,16},{20... | collective-permute-start | bytes 3128 | tf_op jit(solution)/shard_map/ppermute | solution.py:19
  244.1 5.3 %collective-permute-start.22 = (f32[2,1,128]{2,1,0:T(1,128)S(1)}, f32[2,1,128]{2,1,0:T(1,128)S(1)}, u32[]{:S(2)}, u32[]{:S(2)}) collective-permute-start(f32[2,1,128]{2,1,0:T(1,128)S(1)} %get-tuple-element.84), channel_id=1, source_target_pairs={{0,32},{32,64},{64,96},{96,128},{128,160},{160,192},{192,224},{224... | collective-permute-start | bytes 3080 | tf_op jit(solution)/shard_map/ppermute | solution.py:17
  247.2 6.7 %collective-permute-start.23 = (f32[2,1,128]{2,1,0:T(1,128)S(1)}, f32[2,1,128]{2,1,0:T(1,128)S(1)}, u32[]{:S(2)}, u32[]{:S(2)}) collective-permute-start(f32[2,1,128]{2,1,0:T(1,128)S(1)} %get-tuple-element.85), channel_id=1, source_target_pairs={{32,0},{64,32},{96,64},{128,96},{160,128},{192,160},{224,192},{256... | collective-permute-start | bytes 3080 | tf_op jit(solution)/shard_map/ppermute | solution.py:19
  254.0 5.0 %collective-permute-start.24 = (f32[2,130,1]{2,1,0:T(8,128)S(1)}, f32[2,130,1]{2,1,0:T(8,128)S(1)}, u32[]{:S(2)}, u32[]{:S(2)}) collective-permute-start(f32[2,130,1]{2,1,0:T(8,128)S(1)} %get-tuple-element.76), channel_id=1, source_target_pairs={{0,2},{2,4},{4,6},{6,8},{8,10},{10,12},{12,14},{14,16},{16,18},{18... | collective-permute-start | bytes 3128 | tf_op jit(solution)/shard_map/ppermute | solution.py:17
  256.9 22.5 %copy-start.3 = (f32[5,4,128,128]{2,0,3,1:T(8,128)S(1)}, f32[5,4,128,128]{2,0,3,1:T(8,128)}, u32[]{:S(2)}) copy-start(f32[5,4,128,128]{2,0,3,1:T(8,128)} %get-tuple-element.28) | copy-start | bytes 3932164
  256.9 7.7 %collective-permute-start.25 = (f32[2,130,1]{2,1,0:T(8,128)S(1)}, f32[2,130,1]{2,1,0:T(8,128)S(1)}, u32[]{:S(2)}, u32[]{:S(2)}) collective-permute-start(f32[2,130,1]{2,1,0:T(8,128)S(1)} %get-tuple-element.77), channel_id=1, source_target_pairs={{2,0},{4,2},{6,4},{8,6},{10,8},{12,10},{14,12},{16,14},{18,16},{20... | collective-permute-start | bytes 3128 | tf_op jit(solution)/shard_map/ppermute | solution.py:19
  265.3 5.6 %collective-permute-start.26 = (f32[2,1,128]{2,1,0:T(1,128)S(1)}, f32[2,1,128]{2,1,0:T(1,128)S(1)}, u32[]{:S(2)}, u32[]{:S(2)}) collective-permute-start(f32[2,1,128]{2,1,0:T(1,128)S(1)} %get-tuple-element.82), channel_id=1, source_target_pairs={{0,32},{32,64},{64,96},{96,128},{128,160},{160,192},{192,224},{224... | collective-permute-start | bytes 3080 | tf_op jit(solution)/shard_map/ppermute | solution.py:17
  268.9 5.2 %collective-permute-start.27 = (f32[2,1,128]{2,1,0:T(1,128)S(1)}, f32[2,1,128]{2,1,0:T(1,128)S(1)}, u32[]{:S(2)}, u32[]{:S(2)}) collective-permute-start(f32[2,1,128]{2,1,0:T(1,128)S(1)} %get-tuple-element.83), channel_id=1, source_target_pairs={{32,0},{64,32},{96,64},{128,96},{160,128},{192,160},{224,192},{256... | collective-permute-start | bytes 3080 | tf_op jit(solution)/shard_map/ppermute | solution.py:19
  274.3 6.6 %collective-permute-start.28 = (f32[2,130,1]{2,1,0:T(8,128)S(1)}, f32[2,130,1]{2,1,0:T(8,128)S(1)}, u32[]{:S(2)}, u32[]{:S(2)}) collective-permute-start(f32[2,130,1]{2,1,0:T(8,128)S(1)} %get-tuple-element.74), channel_id=1, source_target_pairs={{0,2},{2,4},{4,6},{6,8},{8,10},{10,12},{12,14},{14,16},{16,18},{18... | collective-permute-start | bytes 3128 | tf_op jit(solution)/shard_map/ppermute | solution.py:17
  277.5 7.6 %collective-permute-start.29 = (f32[2,130,1]{2,1,0:T(8,128)S(1)}, f32[2,130,1]{2,1,0:T(8,128)S(1)}, u32[]{:S(2)}, u32[]{:S(2)}) collective-permute-start(f32[2,130,1]{2,1,0:T(8,128)S(1)} %get-tuple-element.75), channel_id=1, source_target_pairs={{2,0},{4,2},{6,4},{8,6},{10,8},{12,10},{14,12},{16,14},{18,16},{20... | collective-permute-start | bytes 3128 | tf_op jit(solution)/shard_map/ppermute | solution.py:19
Sparse Core Ops, SparseCore 0:
  175.3 43.4 all-reduce.2
where the time goes:
time: 295 us; the launch traced here: 293 us
  waiting for transfers between devices  94.7 us (32%)
  starting transfers between devices  91.7 us (31%)
  other arithmetic  47.1 us (16%)
  local copies, waits for them, and re-layouts  44.9 us (15%)
  between operations  14.8 us (5%)
    ppermute x14, starting transfers between devices, extended(): lax.ppermute(tail, axis, [(i, (i + 1) % count) for i in range(ends)])  58.8 us
    psum x1, waiting for transfers between devices, on_device(): exposure = lax.psum(partial_value, 'gz')  42.5 us
    ppermute x14, waiting for transfers between devices, extended(): lax.ppermute(head, axis, [((i + 1) % count, i) for i in range(ends)])  38.9 us
    ppermute x14, starting transfers between devices, extended(): lax.ppermute(head, axis, [((i + 1) % count, i) for i in range(ends)])  26.7 us
    sub x1, other arithmetic, advance(): return center + coefficient * laplace - transport  13.5 us
    ppermute x14, waiting for transfers between devices, extended(): lax.ppermute(tail, axis, [(i, (i + 1) % count) for i in range(ends)])  13.3 us
    slice x10, local copies, waits for them, and re-layouts, extended(): lax.slice_in_dim(cells, cells.shape[dim] - width, cells.shape[dim], axis=...  12.6 us
    reduce_sum x1, other arithmetic, on_device(): partial_value = 0.5 * jnp.sum(fields * weight[None], axis=1)  11.6 us
  transfers between devices with their start and end apart: 31, of which 14 were waited for; matrix products, arithmetic and copies ran while one was open for 24% of the time, Pallas kernels for 0%

commit v1 on v0

v1 whole, which is shorter than its diff:
```python
import jax
import jax.numpy as jnp
from jax import lax
from jax.experimental import pallas as pl
from jax.experimental.pallas import tpu as pltpu
from jax.sharding import PartitionSpec as P

diffusivity = (0.05, 0.04, 0.06, 0.03, 0.045)
SPECIES = 5
L = 4
N = 128
CHUNK = 32
MESH = pl.DeviceIdType.MESH
f32 = jnp.float32


def coefficient_of(s):
    k = jnp.float32(diffusivity[0])
    for i in range(1, SPECIES):
        k = jnp.where(s == i, jnp.float32(diffusivity[i]), k)
    return k


def make_kernel(sizes):
    nx, ny, nz = sizes

    def kernel(
        tracers, wind, band_in, wall_in, exit_in, count_in,
        out_t, out_o, out_f,
        t0, t1, t2, wv, band, floor,
        ylo, yhi, ypack,
        xs, xr, ys, yr,
        m, c0, cx, cy, co,
        e_own, e_oth, er, es, ec, ed,
        sem_t, sem_w, sem_b, sem_f, sem_o,
        z_s, z_r, x_s, x_r, y_s, y_r, m_s, m_r,
        e_s, e_r, er_s, er_r, ec_s, ec_r,
    ):
        gx, gy, gz = lax.axis_index("gx"), lax.axis_index("gy"), lax.axis_index("gz")
        oz = 1 - gz
        gxn, gxp = lax.rem(gx + 1, nx), lax.rem(gx + nx - 1, nx)
        gyn, gyp = lax.rem(gy + 1, ny), lax.rem(gy + ny - 1, ny)
        boundary = (L - 1) * oz

        def layer_of(l):
            return l * oz + (L - 1 - l) * gz

        loads_t = [
            pltpu.make_async_copy(
                tracers.at[:, layer_of(l)], t0.at[:, l + 1, pl.ds(8, N), :], sem_t.at[l]
            )
            for l in range(L)
        ]
        loads_w = [
            pltpu.make_async_copy(wind.at[:, layer_of(l)], wv.at[:, l], sem_w.at[l])
            for l in range(L)
        ]
        loads_f = [
            pltpu.make_async_copy(ref, floor.at[i], sem_f.at[i])
            for i, ref in enumerate((wall_in, exit_in, count_in))
        ]
        load_b = pltpu.make_async_copy(band_in, band, sem_b)
        for c in loads_t:
            c.start()
        for c in loads_f:
            c.start()
        for c in loads_w:
            c.start()
        load_b.start()

        barrier = pltpu.get_barrier_semaphore()
        for dev in (
            (gx, gy, oz), (gxn, gy, gz), (gxp, gy, gz), (gx, gyn, gz), (gx, gyp, gz),
            (gxp, gy, oz), (gx, gyp, oz), (gxp, gyp, gz), (gxp, gyp, oz),
        ):
            pl.semaphore_signal(barrier, inc=1, device_id=dev, device_id_type=MESH)

        def clear(s, carry):
            t0[s, 0, pl.ds(8, N), :] = jnp.zeros((N, N), f32)
            t1[s, 0, pl.ds(8, N), :] = jnp.zeros((N, N), f32)
            return carry

        lax.fori_loop(0, SPECIES, clear, 0)
        pl.semaphore_wait(barrier, 9)

        def z_copy(step, s):
            src = tracers.at[s, boundary] if step == 0 else t1.at[s, L, pl.ds(8, N), :]
            dst = (t0 if step == 0 else t1).at[s, L + 1, pl.ds(8, N), :]
            return pltpu.make_async_remote_copy(
                src, dst, z_s.at[step, s], z_r.at[step, s],
                device_id=(gx, gy, oz), device_id_type=MESH,
            )

        def x_copy(step, d):
            return pltpu.make_async_remote_copy(
                xs.at[step, d], xr.at[step, d], x_s.at[step, d], x_r.at[step, d],
                device_id=((gxn if d == 0 else gxp), gy, gz), device_id_type=MESH,
            )

        def y_copy(step, d):
            return pltpu.make_async_remote_copy(
                ys.at[step, d], yr.at[step, d], y_s.at[step, d], y_r.at[step, d],
                device_id=(gx, (gyn if d == 0 else gyp), gz), device_id_type=MESH,
            )

        def m_copy(d):
            src, dst = ((N, 0), (8, N + 8))[d]
            return pltpu.make_async_remote_copy(
                m.at[:, :, pl.ds(src, 8), :], m.at[:, :, pl.ds(dst, 8), :],
                m_s.at[d], m_r.at[d],
                device_id=((gxn if d == 0 else gxp), gy, gz), device_id_type=MESH,
            )

        def e_copy(s):
            return pltpu.make_async_remote_copy(
                e_own.at[s], e_oth.at[s], e_s.at[s], e_r.at[s],
                device_id=(gx, gy, oz), device_id_type=MESH,
            )

        def er_copy(s, d):
            return pltpu.make_async_remote_copy(
                e_own.at[s, pl.ds(N - 8, 8), :], er.at[d, s],
                er_s.at[d, s], er_r.at[d, s],
                device_id=(gxn, gy, (gz if d == 0 else oz)), device_id_type=MESH,
            )

        def ec_copy(i):
            dev = ((gx, gyn, gz), (gx, gyn, oz), (gxn, gyn, gz), (gxn, gyn, oz))[i]
            return pltpu.make_async_remote_copy(
                es, ec.at[i], ec_s.at[i], ec_r.at[i], device_id=dev, device_id_type=MESH
            )

        z_copy(0, 0).start()
        z_copy(0, 1).start()

        lane = lax.broadcasted_iota(jnp.int32, (CHUNK, N), 1)
        chunks = tuple(range(0, N, CHUNK))

        def pack_x(src, step, s):
            for l in range(L):
                j = s * L + l
                xs[step, 0, pl.ds(j, 1), :] = src[s, l + 1, pl.ds(N + 7, 1), :]
                xs[step, 1, pl.ds(j, 1), :] = src[s, l + 1, pl.ds(8, 1), :]

        def pack_y(src, s):
            for r in chunks:
                low = ypack[0, pl.ds(r, CHUNK), :]
                high = ypack[1, pl.ds(r, CHUNK), :]
                for l in range(L):
                    j = s * L + l
                    c = src[s, l + 1, pl.ds(8 + r, CHUNK), :]
                    low = jnp.where(lane == j, pltpu.roll(c, j + 1, 1), low)
                    high = jnp.where(lane == j, pltpu.roll(c, j, 1), high)
                ypack[0, pl.ds(r, CHUNK), :] = low
                ypack[1, pl.ds(r, CHUNK), :] = high

        def unpack_x(dst, step):
            keep_low = (gx > 0).astype(f32)
            keep_high = (gx < nx - 1).astype(f32)
            for s in range(SPECIES):
                for l in range(L):
                    j = s * L + l
                    dst[s, l + 1, pl.ds(7, 1), :] = xr[step, 0, pl.ds(j, 1), :] * keep_low
                    dst[s, l + 1, pl.ds(N + 8, 1), :] = xr[step, 1, pl.ds(j, 1), :] * keep_high

        def unpack_y(step):
            keep_low = (gy > 0).astype(f32)
            keep_high = (gy < ny - 1).astype(f32)
            filler = jnp.zeros((N - 32, N), f32)
            ylo[...] = jnp.concatenate([yr[step, 0] * keep_low, filler], axis=0).T
            yhi[...] = jnp.concatenate([yr[step, 1] * keep_high, filler], axis=0).T

        def send_y(step):
            ys[step, 0] = ypack[0].T[:32]
            ys[step, 1] = ypack[1].T[:32]
            y_copy(step, 0).start()
            y_copy(step, 1).start()

        flip = (1 - 2 * gz).astype(f32)

        def moved(src, s, l, r, k):
            j = s * L + l
            c = src[s, l + 1, pl.ds(8 + r, CHUNK), :]
            total = c
            u = wv[0, l, pl.ds(r, CHUNK), :]
            total += (k + jnp.maximum(u, 0.0)) * (src[s, l + 1, pl.ds(7 + r, CHUNK), :] - c)
            total += (k - jnp.minimum(u, 0.0)) * (src[s, l + 1, pl.ds(9 + r, CHUNK), :] - c)
            u = wv[1, l, pl.ds(r, CHUNK), :]
            lower = jnp.where(
                lane == 0, pltpu.roll(ylo[pl.ds(r, CHUNK), :], N - j, 1), pltpu.roll(c, 1, 1)
            )
            upper = jnp.where(
                lane == N - 1, pltpu.roll(yhi[pl.ds(r, CHUNK), :], N - 1 - j, 1),
                pltpu.roll(c, N - 1, 1),
            )
            total += (k + jnp.maximum(u, 0.0)) * (lower - c)
            total += (k - jnp.minimum(u, 0.0)) * (upper - c)
            u = wv[2, l, pl.ds(r, CHUNK), :] * flip
            total += (k + jnp.maximum(u, 0.0)) * (src[s, l, pl.ds(8 + r, CHUNK), :] - c)
            total += (k - jnp.minimum(u, 0.0)) * (src[s, l + 2, pl.ds(8 + r, CHUNK), :] - c)
            return total

        for c in loads_t:
            c.wait()
        for s in range(SPECIES):
            pack_x(t0, 0, s)
        x_copy(0, 0).start()
        x_copy(0, 1).start()
        for s in range(2, SPECIES):
            z_copy(0, s).start()
        for c in loads_f:
            c.wait()
        passable = 1.0 - floor[0].astype(f32)
        leave = 1.0 - 0.5 * floor[1].astype(f32)
        start = 0.25 * floor[2].astype(f32) * passable
        m[0, 0, pl.ds(8, N), :] = start
        m[1, 0, pl.ds(8, N), :] = passable
        m[2, 0, pl.ds(8, N), :] = leave
        wide = lax.broadcasted_iota(jnp.int32, (N, N), 1)
        low = jnp.zeros((N, N), f32)
        high = jnp.zeros((N, N), f32)
        for i, field in enumerate((start, passable, leave)):
            a = 20 + 4 * i
            inside = (wide >= a) & (wide < a + 4)
            low = jnp.where(inside, pltpu.roll(field, a + 4, 1), low)
            high = jnp.where(inside, pltpu.roll(field, a, 1), high)
        ypack[0] = low
        ypack[1] = high

        def pack_y0(s, carry):
            pack_y(t0, s)
            return carry

        lax.fori_loop(0, SPECIES, pack_y0, 0)
        send_y(0)
        for c in loads_w:
            c.wait()
        load_b.wait()
        x_copy(0, 0).wait_recv()
        x_copy(0, 1).wait_recv()
        unpack_x(t0, 0)
        y_copy(0, 0).wait_recv()
        y_copy(0, 1).wait_recv()
        unpack_y(0)

        for i in range(3):
            a = 20 + 4 * i
            above = pltpu.roll(yhi[...], N - a, 1)
            below = pltpu.roll(ylo[...], N - 4 - a, 1)
            m[i, 1, pl.ds(8, N), :] = jnp.where(
                wide < 4, above, jnp.where(wide >= N - 4, below, 0.0)
            )
        m_copy(0).start()
        m_copy(1).start()

        def first(s, carry):
            k = coefficient_of(s)
            z_copy(0, s).wait_recv()
            for l in (L - 1, 0, 1, 2):
                for r in chunks:
                    t1[s, l + 1, pl.ds(8 + r, CHUNK), :] = moved(t0, s, l, r, k)
            z_copy(1, s).start()
            pack_x(t1, 1, s)
            pack_y(t1, s)
            return carry

        lax.fori_loop(0, SPECIES, first, 0)
        x_copy(1, 0).start()
        x_copy(1, 1).start()
        send_y(1)

        m_copy(0).wait()
        m_copy(1).wait()
        rows = N + 16
        lane_m = lax.broadcasted_iota(jnp.int32, (rows, N), 1)
        row_m = lax.broadcasted_iota(jnp.int32, (rows, N), 0)
        first_row = jnp.where(gx > 0, 0, 8)
        last_row = jnp.where(gx < nx - 1, rows, N + 8)
        inside = (row_m >= first_row) & (row_m < last_row)

        def y_lower(a, b):
            ra, rb = pltpu.roll(a, 1, 1), pltpu.roll(b, 1, 1)
            return jnp.where(lane_m == 0, rb, ra), jnp.where(lane_m == 0, ra, rb)

        def y_upper(a, b):
            ra, rb = pltpu.roll(a, N - 1, 1), pltpu.roll(b, N - 1, 1)
            return jnp.where(lane_m == N - 1, rb, ra), jnp.where(lane_m == N - 1, ra, rb)

        occ = [jnp.where(inside, m[0, i], 0.0) for i in range(2)]
        free = [jnp.where(inside, m[1, i], 0.0) for i in range(2)]
        out = [m[2, i] for i in range(2)]
        free_y = y_upper(*free)
        px = [0.25 * free[i] * pltpu.roll(free[i], rows - 1, 0) for i in range(2)]
        py = [0.15 * free[i] * free_y[i] for i in range(2)]
        for step in range(4):
            occ_yu = y_upper(*occ)
            occ_yl = y_lower(*occ)
            gate_x = [px[i] * (1.0 - pltpu.roll(occ[i], rows - 1, 0)) for i in range(2)]
            gate_y = [py[i] * (1.0 - occ_yu[i]) for i in range(2)]
            gate_yl = y_lower(*gate_y)
            after = []
            for i in range(2):
                stay = out[i] * (1.0 - gate_x[i] - gate_y[i])
                in_x = out[i] * pltpu.roll(gate_x[i], 1, 0)
                in_y = out[i] * gate_yl[i]
                c0[step, i] = stay[: N + 8]
                cx[step, i] = in_x[: N + 8]
                cy[step, i] = in_y[: N + 8]
                co[step, i] = (out[i] * occ[i])[: N + 8]
                after.append(stay * occ[i] + in_x * pltpu.roll(occ[i], 1, 0) + in_y * occ_yl[i])
            occ = after
        out_o[...] = occ[0][8 : N + 8]

        x_copy(1, 0).wait_recv()
        x_copy(1, 1).wait_recv()
        unpack_x(t1, 1)
        y_copy(1, 0).wait_recv()
        y_copy(1, 1).wait_recv()
        unpack_y(1)

        def out_copy(s, l):
            return pltpu.make_async_copy(t2.at[s, l], out_t.at[s, layer_of(l)], sem_o.at[s, l])

        def in_band(l, r):
            b = band[pl.ds(r, CHUNK), :]
            layer = l * oz + (2 * L - 1 - l) * gz
            return (b == layer) | (b == layer - 1)

        def second(s, carry):
            k = coefficient_of(s)
            for r in chunks:
                acc = jnp.zeros((CHUNK, N), f32)
                for l in range(L - 1):
                    new = moved(t1, s, l, r, k)
                    t2[s, l, pl.ds(r, CHUNK), :] = new
                    acc += jnp.where(in_band(l, r), 0.5 * new, 0.0)
                e_own[s, pl.ds(r, CHUNK), :] = acc
            z_copy(1, s).wait_recv()
            for r in chunks:
                new = moved(t1, s, L - 1, r, k)
                t2[s, L - 1, pl.ds(r, CHUNK), :] = new
                e_own[s, pl.ds(r, CHUNK), :] += jnp.where(in_band(L - 1, r), 0.5 * new, 0.0)
            for l in range(L):
                out_copy(s, l).start()
            er_copy(s, 0).start()
            er_copy(s, 1).start()
            e_copy(s).start()
            return carry

        lax.fori_loop(0, SPECIES, second, 0)
        strip = jnp.zeros((N, N), f32)
        for s in range(SPECIES):
            mine = (wide >= 3 * s) & (wide < 3 * s + 3)
            strip = jnp.where(mine, pltpu.roll(e_own[s], 3 * s + 3, 1), strip)
        es[...] = strip.T[:16]
        for i in range(4):
            ec_copy(i).start()

        def rate_of(co_, co2, hcn, o2, heat):
            return (
                0.3 * co_ * jnp.exp(0.3 * co2) + 0.2 * hcn
                + 0.1 * (2.0 - o2) * (2.0 - o2) + 0.1 * heat * heat
            )

        for s in range(SPECIES):
            er_copy(s, 0).wait_recv()
            er_copy(s, 1).wait_recv()
        edge = rate_of(*[er[0, s] + er[1, s] for s in range(SPECIES)])
        for i in range(4):
            ec_copy(i).wait_recv()
        filler = jnp.zeros((N - 16, N), f32)
        side = jnp.concatenate([ec[0] + ec[1], filler], axis=0).T
        corner = jnp.concatenate([ec[2] + ec[3], filler], axis=0).T[N - 8 :]
        side = jnp.concatenate([corner, side], axis=0)
        side = rate_of(*[pltpu.roll(side, N - 3 - 3 * s, 1) for s in range(SPECIES)])
        for s in range(SPECIES):
            e_copy(s).wait_recv()
        middle = rate_of(*[e_own[s] + e_oth[s] for s in range(SPECIES)])
        lane_d = lax.broadcasted_iota(jnp.int32, (N + 8, N), 1)
        rate = [
            jnp.concatenate([edge, middle], axis=0),
            jnp.where(lane_d >= N - 3, side, 0.0),
        ]
        dose = [co[0, i] * rate[i] for i in range(2)]
        for step in range(1, 4):
            ra, rb = pltpu.roll(dose[0], 1, 1), pltpu.roll(dose[1], 1, 1)
            left = (jnp.where(lane_d == 0, rb, ra), jnp.where(lane_d == 0, ra, rb))
            dose = [
                c0[step, i] * dose[i] + cx[step, i] * pltpu.roll(dose[i], 1, 0)
                + cy[step, i] * left[i] + co[step, i] * rate[i]
                for i in range(2)
            ]
        out_f[...] = dose[0][8:]

        for step in range(2):
            for d in range(2):
                x_copy(step, d).wait_send()
                y_copy(step, d).wait_send()

        def finish(s, carry):
            z_copy(0, s).wait_send()
            z_copy(1, s).wait_send()
            e_copy(s).wait_send()
            er_copy(s, 0).wait_send()
            er_copy(s, 1).wait_send()
            for l in range(L):
                out_copy(s, l).wait()
            return carry

        lax.fori_loop(0, SPECIES, finish, 0)
        for i in range(4):
            ec_copy(i).wait_send()

    return kernel


def solution(mesh):
    sizes = tuple(mesh.shape[name] for name in ("gx", "gy", "gz"))

    def on_device(tracers, wind_field, band_layer, wall_mask, exit_mask, occupant_count):
        floor = jax.ShapeDtypeStruct((N, N), f32)
        hbm = pl.BlockSpec(memory_space=pl.ANY)
        vmem = pl.BlockSpec(memory_space=pltpu.VMEM)
        V = pltpu.VMEM
        D = pltpu.SemaphoreType.DMA
        return pl.pallas_call(
            make_kernel(sizes),
            out_shape=(jax.ShapeDtypeStruct((SPECIES, L, N, N), f32), floor, floor),
            in_specs=[hbm] * 6,
            out_specs=(hbm, vmem, vmem),
            scratch_shapes=[
                V((SPECIES, L + 2, N + 16, N), f32),
                V((SPECIES, L + 2, N + 16, N), f32),
                V((SPECIES, L, N, N), f32),
                V((3, L, N, N), f32),
                V((N, N), jnp.int32),
                V((3, N, N), jnp.int32),
                V((N, N), f32), V((N, N), f32), V((2, N, N), f32),
                V((2, 2, 24, N), f32), V((2, 2, 24, N), f32),
                V((2, 2, 32, N), f32), V((2, 2, 32, N), f32),
                V((3, 2, N + 16, N), f32),
                V((4, 2, N + 8, N), f32), V((4, 2, N + 8, N), f32),
                V((4, 2, N + 8, N), f32), V((4, 2, N + 8, N), f32),
                V((SPECIES, N, N), f32), V((SPECIES, N, N), f32),
                V((2, SPECIES, 8, N), f32),
                V((16, N), f32), V((4, 16, N), f32), V((8, N), f32),
                D((L,)), D((L,)), D, D((3,)), D((SPECIES, L)),
                D((2, SPECIES)), D((2, SPECIES)),
                D((2, 2)), D((2, 2)), D((2, 2)), D((2, 2)), D((2,)), D((2,)),
                D((SPECIES,)), D((SPECIES,)), D((2, SPECIES)), D((2, SPECIES)),
                D((4,)), D((4,)),
            ],
            compiler_params=pltpu.CompilerParams(
                collective_id=0, has_side_effects=True, vmem_limit_bytes=48 * 1024 * 1024
            ),
        )(tracers, wind_field, band_layer, wall_mask, exit_mask, occupant_count)

    return jax.shard_map(
        on_device,
        mesh=mesh,
        in_specs=(
            P(None, "gz", "gx", "gy"),
            P(None, "gz", "gx", "gy"),
            P("gx", "gy"),
            P("gx", "gy"),
            P("gx", "gy"),
            P("gx", "gy"),
        ),
        out_specs=(P(None, "gz", "gx", "gy"), P("gx", "gy"), P("gx", "gy")),
        check_vma=False,
    )
```

time: 295 us -> 51 us (0.17)
  the two profiles are of different devices: /device:TPU:155 before, /device:TPU:1 now
where the time goes in v1:
time: 51 us; the launch traced here: 50.6 us
  Pallas kernels  41.9 us (82%)
  local copies, waits for them, and re-layouts  8.11 us (16%)
  between operations  0.65 us (1%)
    pallas_call x1, Pallas kernels, on_device(): pl.pallas_call(make_kernel(sizes), out_shape=(jax.ShapeDtypeStruct((SPECI...  41.9 us
    unnamed x15, local copies, waits for them, and re-layouts  8.11 us

profile of v1, /device:TPU:1, one launch (start us, length us, event | category | flops | bytes accessed | tf_op | source)
XLA Modules:
  0.0 50.6 jit_solution(5146124482601327759)
XLA Ops:
  0.6 0.0 copy-start
  0.6 1.3 %copy-done = f32[5,4,128,128]{3,2,1,0:T(8,128)S(1)} copy-done((f32[5,4,128,128]{3,2,1,0:T(8,128)S(1)}, f32[5,4,128,128]{3,2,1,0:T(8,128)}, u32[]{:S(2)}) %copy-start) | copy-done | bytes 1310744
  1.9 0.0 copy-start.1
  2.0 1.1 %copy-done.1 = f32[3,4,128,128]{3,2,1,0:T(8,128)S(1)} copy-done((f32[3,4,128,128]{3,2,1,0:T(8,128)S(1)}, f32[3,4,128,128]{3,2,1,0:T(8,128)}, u32[]{:S(2)}) %copy-start.1) | copy-done | bytes 786456
  3.1 0.0 copy-start.2
  3.1 0.8 %copy-done.2 = s32[128,128]{1,0:T(8,128)S(1)} copy-done((s32[128,128]{1,0:T(8,128)S(1)}, s32[128,128]{1,0:T(8,128)}, u32[]{:S(2)}) %copy-start.2) | copy-done | bytes 65560
  3.9 0.0 copy-start.3
  3.9 0.8 %copy-done.3 = s32[128,128]{1,0:T(8,128)S(1)} copy-done((s32[128,128]{1,0:T(8,128)S(1)}, s32[128,128]{1,0:T(8,128)}, u32[]{:S(2)}) %copy-start.3) | copy-done | bytes 65560
  4.8 0.0 copy-start.4
  4.8 0.8 %copy-done.4 = s32[128,128]{1,0:T(8,128)S(1)} copy-done((s32[128,128]{1,0:T(8,128)S(1)}, s32[128,128]{1,0:T(8,128)}, u32[]{:S(2)}) %copy-start.4) | copy-done | bytes 65560
  5.6 0.0 copy-start.5
  5.6 0.8 %copy-done.5 = s32[128,128]{1,0:T(8,128)S(1)} copy-done((s32[128,128]{1,0:T(8,128)S(1)}, s32[128,128]{1,0:T(8,128)}, u32[]{:S(2)}) %copy-start.5) | copy-done | bytes 65560
  6.4 41.9 %shard_map.85 = (f32[5,4,128,128]{3,2,1,0:T(8,128)S(1)}, f32[128,128]{1,0:T(8,128)S(1)}, f32[128,128]{1,0:T(8,128)S(1)}) custom-call(f32[5,4,128,128]{3,2,1,0:T(8,128)S(1)} %copy-done, f32[3,4,128,128]{3,2,1,0:T(8,128)S(1)} %copy-done.1, s32[128,128]{1,0:T(8,128)S(1)} %copy-done.2, s32[128,128]{1,0:T(8,128)S(1)} %copy-done.3, s32[128,128]{1,0:T(8,128)S(1)} %copy-done.4, ...), custom_call_target="tpu_custom_call" | custom-call | tf_op jit(solution)/shard_map/pallas_call | solution.py:426
  48.3 1.1 %copy.12 = f32[5,4,128,128]{3,2,1,0:T(8,128)} copy(f32[5,4,128,128]{3,2,1,0:T(8,128)S(1)} %get-tuple-element.6) | data formatting | bytes 2621440
  49.4 0.6 %copy.13 = f32[128,128]{1,0:T(8,128)} copy(f32[128,128]{1,0:T(8,128)S(1)} %get-tuple-element.7) | data formatting | bytes 131072
  50.0 0.6 %copy.14 = f32[128,128]{1,0:T(8,128)} copy(f32[128,128]{1,0:T(8,128)S(1)} %get-tuple-element.8) | data formatting | bytes 131072
Async XLA Ops:
  0.6 1.3 %copy-start = (f32[5,4,128,128]{3,2,1,0:T(8,128)S(1)}, f32[5,4,128,128]{3,2,1,0:T(8,128)}, u32[]{:S(2)}) copy-start(f32[5,4,128,128]{3,2,1,0:T(8,128)} %tracers.1) | copy-start | bytes 3932164
  1.9 1.1 %copy-start.1 = (f32[3,4,128,128]{3,2,1,0:T(8,128)S(1)}, f32[3,4,128,128]{3,2,1,0:T(8,128)}, u32[]{:S(2)}) copy-start(f32[3,4,128,128]{3,2,1,0:T(8,128)} %wind.1) | copy-start | bytes 2359300
  3.1 0.8 %copy-start.2 = (s32[128,128]{1,0:T(8,128)S(1)}, s32[128,128]{1,0:T(8,128)}, u32[]{:S(2)}) copy-start(s32[128,128]{1,0:T(8,128)} %band_in.1) | copy-start | bytes 196612
  3.9 0.8 %copy-start.3 = (s32[128,128]{1,0:T(8,128)S(1)}, s32[128,128]{1,0:T(8,128)}, u32[]{:S(2)}) copy-start(s32[128,128]{1,0:T(8,128)} %wall_in.1) | copy-start | bytes 196612
  4.8 0.8 %copy-start.4 = (s32[128,128]{1,0:T(8,128)S(1)}, s32[128,128]{1,0:T(8,128)}, u32[]{:S(2)}) copy-start(s32[128,128]{1,0:T(8,128)} %exit_in.1) | copy-start | bytes 196612
  5.6 0.8 %copy-start.5 = (s32[128,128]{1,0:T(8,128)S(1)}, s32[128,128]{1,0:T(8,128)}, u32[]{:S(2)}) copy-start(s32[128,128]{1,0:T(8,128)} %count_in.1) | copy-start | bytes 196612

commit v2 on v1

v2 whole, which is shorter than its diff:
```python
import jax
import jax.numpy as jnp
from jax import lax
from jax.experimental import pallas as pl
from jax.experimental.pallas import tpu as pltpu
from jax.sharding import PartitionSpec as P

diffusivity = (0.05, 0.04, 0.06, 0.03, 0.045)
SPECIES = 5
L = 4
N = 128
CHUNK = 32
HOLD = 3
MESH = pl.DeviceIdType.MESH
f32 = jnp.float32


def coefficient_of(s):
    k = jnp.float32(diffusivity[0])
    for i in range(1, SPECIES):
        k = jnp.where(s == i, jnp.float32(diffusivity[i]), k)
    return k


def make_kernel(sizes):
    nx, ny, nz = sizes

    def kernel(
        tracers, wind, band_in, wall_in, exit_in, count_in,
        out_t, out_o, out_f,
        t0, t1, wv, band, floor,
        yedge, ypack, ys, yr,
        m, c0, cx, cy, co,
        e_own, e_oth, er, es, ec,
        sem_t, sem_w, sem_b, sem_f,
        z_s, z_r, x_s, x_r, y_s, y_r, m_s, m_r,
        e_s, e_r, er_s, er_r, ec_s, ec_r,
    ):
        gx, gy, gz = lax.axis_index("gx"), lax.axis_index("gy"), lax.axis_index("gz")
        oz = 1 - gz
        gxn, gxp, gyn, gyp = gx + 1, gx - 1, gy + 1, gy - 1
        has_xn, has_xp, has_yn, has_yp = gx < nx - 1, gx > 0, gy < ny - 1, gy > 0
        x_has = (has_xn, has_xp)
        y_has = (has_yn, has_yp)
        boundary = (L - 1) * oz

        def layer_of(l):
            return l * oz + (L - 1 - l) * gz

        loads_t = [
            pltpu.make_async_copy(
                tracers.at[:, layer_of(l)], t0.at[:, l + 1, pl.ds(8, N), :], sem_t.at[l]
            )
            for l in range(L)
        ]
        loads_w = [
            pltpu.make_async_copy(wind.at[:, layer_of(l)], wv.at[:, l], sem_w.at[l])
            for l in range(L)
        ]
        loads_f = [
            pltpu.make_async_copy(ref, floor.at[i], sem_f.at[i])
            for i, ref in enumerate((wall_in, exit_in, count_in))
        ]
        load_b = pltpu.make_async_copy(band_in, band, sem_b)
        for c in loads_t:
            c.start()
        for c in loads_f:
            c.start()
        for c in loads_w:
            c.start()
        load_b.start()

        barrier = pltpu.get_barrier_semaphore()

        def greet(*devs):
            for dev in devs:
                pl.semaphore_signal(barrier, inc=1, device_id=dev, device_id_type=MESH)

        greet((gx, gy, oz))
        pl.when(has_xn)(lambda: greet((gxn, gy, gz)))
        pl.when(has_xp)(lambda: greet((gxp, gy, gz), (gxp, gy, oz)))
        pl.when(has_yn)(lambda: greet((gx, gyn, gz)))
        pl.when(has_yp)(lambda: greet((gx, gyp, gz), (gx, gyp, oz)))
        pl.when(has_xp & has_yp)(lambda: greet((gxp, gyp, gz), (gxp, gyp, oz)))

        def clear(s, carry):
            t0[s, 0, pl.ds(8, N), :] = jnp.zeros((N, N), f32)
            t1[s, 0, pl.ds(8, N), :] = jnp.zeros((N, N), f32)
            return carry

        lax.fori_loop(0, SPECIES, clear, 0)

        def clear_rows(row):
            for s in range(SPECIES):
                for l in range(1, L + 1):
                    t0[s, l, pl.ds(row, 1), :] = jnp.zeros((1, N), f32)
                    t1[s, l, pl.ds(row, 1), :] = jnp.zeros((1, N), f32)

        er[:, :, pl.ds(0, 5), :] = jnp.zeros((2, SPECIES, 5, N), f32)
        m[:, :, pl.ds(0, 4), :] = jnp.zeros((3, 2, 4, N), f32)
        m[:, :, pl.ds(N + 12, 4), :] = jnp.zeros((3, 2, 4, N), f32)

        @pl.when(jnp.logical_not(has_xp))
        def _():
            clear_rows(7)
            er[:, :, pl.ds(5, 3), :] = jnp.zeros((2, SPECIES, 3, N), f32)
            m[:, :, pl.ds(4, 4), :] = jnp.zeros((3, 2, 4, N), f32)

        @pl.when(jnp.logical_not(has_xn))
        def _():
            clear_rows(N + 8)
            m[:, :, pl.ds(N + 8, 4), :] = jnp.zeros((3, 2, 4, N), f32)

        @pl.when(jnp.logical_not(has_yp))
        def _():
            yr[0, 0] = jnp.zeros((72, N), f32)
            yr[1, 0] = jnp.zeros((72, N), f32)
            ec[0] = jnp.zeros((16, N), f32)
            ec[1] = jnp.zeros((16, N), f32)

        @pl.when(jnp.logical_not(has_yn))
        def _():
            yr[0, 1] = jnp.zeros((72, N), f32)
            yr[1, 1] = jnp.zeros((72, N), f32)

        @pl.when(jnp.logical_not(has_xp & has_yp))
        def _():
            ec[2] = jnp.zeros((16, N), f32)
            ec[3] = jnp.zeros((16, N), f32)

        one = lambda flag: flag.astype(jnp.int32)
        pl.semaphore_wait(
            barrier,
            1 + 2 * one(has_xn) + one(has_xp) + 2 * one(has_yn) + one(has_yp)
            + 2 * one(has_xn) * one(has_yn),
        )

        def z_copy(step, s):
            src = tracers.at[s, boundary] if step == 0 else t1.at[s, L, pl.ds(8, N), :]
            dst = (t0 if step == 0 else t1).at[s, L + 1, pl.ds(8, N), :]
            return pltpu.make_async_remote_copy(
                src, dst, z_s.at[step, s], z_r.at[step, s],
                device_id=(gx, gy, oz), device_id_type=MESH,
            )

        def x_copies(step, d):
            dev = ((gxn if d == 0 else gxp), gy, gz)
            src, dst = ((N + 7, 7), (8, N + 8))[d]
            if step == 1:
                return [
                    pltpu.make_async_remote_copy(
                        t1.at[:, pl.ds(1, L), pl.ds(src, 1), :],
                        t1.at[:, pl.ds(1, L), pl.ds(dst, 1), :],
                        x_s.at[1, d, 0], x_r.at[1, d, 0],
                        device_id=dev, device_id_type=MESH,
                    )
                ]
            return [
                pltpu.make_async_remote_copy(
                    tracers.at[:, layer_of(l), pl.ds(src - 8, 1), :],
                    t0.at[:, l + 1, pl.ds(dst, 1), :],
                    x_s.at[0, d, l], x_r.at[0, d, l],
                    device_id=dev, device_id_type=MESH,
                )
                for l in range(L)
            ]

        def y_copy(step, d):
            rows = 72 if step == 0 else 48
            return pltpu.make_async_remote_copy(
                ys.at[step, pl.ds(0, rows), :], yr.at[step, d, pl.ds(0, rows), :],
                y_s.at[step, d], y_r.at[step, d],
                device_id=(gx, (gyn if d == 0 else gyp), gz), device_id_type=MESH,
            )

        def m_copy(d):
            src, dst = ((N + 4, 4), (8, N + 8))[d]
            return pltpu.make_async_remote_copy(
                m.at[:, :, pl.ds(src, 4), :], m.at[:, :, pl.ds(dst, 4), :],
                m_s.at[d], m_r.at[d],
                device_id=((gxn if d == 0 else gxp), gy, gz), device_id_type=MESH,
            )

        def send_x(step):
            for d in range(2):
                @pl.when(x_has[d])
                def _():
                    for c in x_copies(step, d):
                        c.start()

        def recv_x(step):
            for d in range(2):
                @pl.when(x_has[1 - d])
                def _():
                    for c in x_copies(step, d):
                        c.wait_recv()

        def recv_y(step):
            for d in range(2):
                pl.when(y_has[1 - d])(lambda: y_copy(step, d).wait_recv())

        def e_copy(s):
            return pltpu.make_async_remote_copy(
                e_own.at[s], e_oth.at[s], e_s.at[s], e_r.at[s],
                device_id=(gx, gy, oz), device_id_type=MESH,
            )

        def er_copy(s, d):
            return pltpu.make_async_remote_copy(
                e_own.at[s, pl.ds(N - 3, 3), :], er.at[d, s, pl.ds(5, 3), :],
                er_s.at[d, s], er_r.at[d, s],
                device_id=(gxn, gy, (gz if d == 0 else oz)), device_id_type=MESH,
            )

        def ec_copy(i):
            dev = ((gx, gyn, gz), (gx, gyn, oz), (gxn, gyn, gz), (gxn, gyn, oz))[i]
            return pltpu.make_async_remote_copy(
                es, ec.at[i], ec_s.at[i], ec_r.at[i], device_id=dev, device_id_type=MESH
            )

        send_x(0)
        z_copy(0, 0).start()
        z_copy(0, 1).start()

        lane = lax.broadcasted_iota(jnp.int32, (CHUNK, N), 1)
        chunks = tuple(range(0, N, CHUNK))

        def pack_y(src, s):
            for r in chunks:
                acc = ypack[pl.ds(r, CHUNK), :]
                for l in range(L):
                    j = 2 * (s * L + l)
                    c = src[s, l + 1, pl.ds(8 + r, CHUNK), :]
                    here = (lane == j + 1) | (lane == j + 2)
                    acc = jnp.where(here, pltpu.roll(c, j + 2, 1), acc)
                ypack[pl.ds(r, CHUNK), :] = acc

        def unpack_y(step):
            row = lax.broadcasted_iota(jnp.int32, (72, N), 0)
            before = yr[step, 0]
            after = yr[step, 1]
            after = jnp.where(row < 48, pltpu.roll(after, 70, 0), after)
            from_before = ((row < 48) & ((row & 1) == 1)) | ((row >= 48) & ((row & 7) < 4))
            both = jnp.where(from_before, before, after)
            yedge[...] = jnp.concatenate([both, jnp.zeros((N - 72, N), f32)], axis=0).T

        def send_y(step):
            ys[step] = ypack[...].T[:72]
            for d in range(2):
                pl.when(y_has[d])(lambda: y_copy(step, d).start())

        flip = (1 - 2 * gz).astype(f32)

        def moved(src, s, l, r, k):
            j = s * L + l
            c = src[s, l + 1, pl.ds(8 + r, CHUNK), :]
            total = c
            u = wv[0, l, pl.ds(r, CHUNK), :]
            total += (k + jnp.maximum(u, 0.0)) * (src[s, l + 1, pl.ds(7 + r, CHUNK), :] - c)
            total += (k - jnp.minimum(u, 0.0)) * (src[s, l + 1, pl.ds(9 + r, CHUNK), :] - c)
            u = wv[1, l, pl.ds(r, CHUNK), :]
            edge = pltpu.roll(yedge[pl.ds(r, CHUNK), :], N - 1 - 2 * j, 1)
            lower = jnp.where(lane == 0, edge, pltpu.roll(c, 1, 1))
            upper = jnp.where(lane == N - 1, edge, pltpu.roll(c, N - 1, 1))
            total += (k + jnp.maximum(u, 0.0)) * (lower - c)
            total += (k - jnp.minimum(u, 0.0)) * (upper - c)
            u = wv[2, l, pl.ds(r, CHUNK), :] * flip
            total += (k + jnp.maximum(u, 0.0)) * (src[s, l, pl.ds(8 + r, CHUNK), :] - c)
            total += (k - jnp.minimum(u, 0.0)) * (src[s, l + 2, pl.ds(8 + r, CHUNK), :] - c)
            return total

        for c in loads_f:
            c.wait()
        passable = 1.0 - floor[0].astype(f32)
        leave = 1.0 - 0.5 * floor[1].astype(f32)
        start = 0.25 * floor[2].astype(f32) * passable
        m[0, 0, pl.ds(8, N), :] = start
        m[1, 0, pl.ds(8, N), :] = passable
        m[2, 0, pl.ds(8, N), :] = leave
        wide = lax.broadcasted_iota(jnp.int32, (N, N), 1)
        acc = jnp.zeros((N, N), f32)
        for i, field in enumerate((start, passable, leave)):
            a = 48 + 8 * i
            acc = jnp.where((wide >= a) & (wide < a + 8), pltpu.roll(field, a + 4, 1), acc)
        ypack[...] = acc
        for c in loads_t:
            c.wait()

        def pack_y0(s, carry):
            pack_y(t0, s)
            return carry

        lax.fori_loop(0, SPECIES, pack_y0, 0)
        send_y(0)
        for s in range(2, SPECIES):
            z_copy(0, s).start()
        for c in loads_w:
            c.wait()
        load_b.wait()
        recv_y(0)
        unpack_y(0)

        for i in range(3):
            beside = pltpu.roll(yedge[...], N - 52 - 8 * i, 1)
            m[i, 1, pl.ds(8, N), :] = jnp.where((wide < 4) | (wide >= N - 4), beside, 0.0)
        for d in range(2):
            pl.when(x_has[d])(lambda: m_copy(d).start())
        recv_x(0)

        def first(s, carry):
            k = coefficient_of(s)
            z_copy(0, s).wait_recv()
            for l in (L - 1, 0, 1, 2):
                for r in chunks:
                    t1[s, l + 1, pl.ds(8 + r, CHUNK), :] = moved(t0, s, l, r, k)

            @pl.when(s < 2)
            def _():
                z_copy(1, s).start()

            pack_y(t1, s)
            return carry

        lax.fori_loop(0, SPECIES, first, 0)
        send_x(1)
        send_y(1)
        for s in range(2, SPECIES):
            z_copy(1, s).start()

        for d in range(2):
            pl.when(x_has[1 - d])(lambda: m_copy(d).wait_recv())
        rows = N + 16
        lane_m = lax.broadcasted_iota(jnp.int32, (rows, N), 1)

        def y_lower(a, b):
            ra, rb = pltpu.roll(a, 1, 1), pltpu.roll(b, 1, 1)
            return jnp.where(lane_m == 0, rb, ra), jnp.where(lane_m == 0, ra, rb)

        def y_upper(a, b):
            ra, rb = pltpu.roll(a, N - 1, 1), pltpu.roll(b, N - 1, 1)
            return jnp.where(lane_m == N - 1, rb, ra), jnp.where(lane_m == N - 1, ra, rb)

        occ = [m[0, i] for i in range(2)]
        free = [m[1, i] for i in range(2)]
        out = [m[2, i] for i in range(2)]
        free_y = y_upper(*free)
        px = [0.25 * free[i] * pltpu.roll(free[i], rows - 1, 0) for i in range(2)]
        py = [0.15 * free[i] * free_y[i] for i in range(2)]
        for step in range(4):
            occ_yu = y_upper(*occ)
            occ_yl = y_lower(*occ)
            gate_x = [px[i] * (1.0 - pltpu.roll(occ[i], rows - 1, 0)) for i in range(2)]
            gate_y = [py[i] * (1.0 - occ_yu[i]) for i in range(2)]
            gate_yl = y_lower(*gate_y)
            after = []
            for i in range(2):
                stay = out[i] * (1.0 - gate_x[i] - gate_y[i])
                in_x = out[i] * pltpu.roll(gate_x[i], 1, 0)
                in_y = out[i] * gate_yl[i]
                c0[step, i] = stay[: N + 8]
                cx[step, i] = in_x[: N + 8]
                cy[step, i] = in_y[: N + 8]
                co[step, i] = (out[i] * occ[i])[: N + 8]
                after.append(stay * occ[i] + in_x * pltpu.roll(occ[i], 1, 0) + in_y * occ_yl[i])
            occ = after
        out_o[...] = occ[0][8 : N + 8]

        recv_x(1)
        recv_y(1)
        unpack_y(1)

        def in_band(l, r):
            b = band[pl.ds(r, CHUNK), :]
            layer = l * oz + (2 * L - 1 - l) * gz
            return (b == layer) | (b == layer - 1)

        def second(s, carry):
            k = coefficient_of(s)
            for r in chunks:
                acc = jnp.zeros((CHUNK, N), f32)
                for l in range(L - 1):
                    new = moved(t1, s, l, r, k)
                    out_t[s, layer_of(l), pl.ds(r, CHUNK), :] = new
                    acc += jnp.where(in_band(l, r), 0.5 * new, 0.0)
                e_own[s, pl.ds(r, CHUNK), :] = acc
            z_copy(1, s).wait_recv()
            for r in chunks:
                new = moved(t1, s, L - 1, r, k)
                out_t[s, boundary, pl.ds(r, CHUNK), :] = new
                e_own[s, pl.ds(r, CHUNK), :] += jnp.where(in_band(L - 1, r), 0.5 * new, 0.0)

            @pl.when(has_xn)
            def _():
                er_copy(s, 0).start()
                er_copy(s, 1).start()

            @pl.when(s < HOLD)
            def _():
                e_copy(s).start()

            return carry

        lax.fori_loop(0, SPECIES, second, 0)
        strip = jnp.zeros((N, N), f32)
        for s in range(SPECIES):
            mine = (wide >= 3 * s) & (wide < 3 * s + 3)
            strip = jnp.where(mine, pltpu.roll(e_own[s], 3 * s + 3, 1), strip)
        es[...] = strip.T[:16]
        ec_to = (has_yn, has_yn, has_xn & has_yn, has_xn & has_yn)
        ec_from = (has_yp, has_yp, has_xp & has_yp, has_xp & has_yp)
        for i in range(4):
            pl.when(ec_to[i])(lambda: ec_copy(i).start())
        for s in range(HOLD, SPECIES):
            e_copy(s).start()

        def rate_of(co_, co2, hcn, o2, heat):
            return (
                0.3 * co_ * jnp.exp(0.3 * co2) + 0.2 * hcn
                + 0.1 * (2.0 - o2) * (2.0 - o2) + 0.1 * heat * heat
            )

        @pl.when(has_xp)
        def _():
            for s in range(SPECIES):
                er_copy(s, 0).wait_recv()
                er_copy(s, 1).wait_recv()

        edge = rate_of(*[er[0, s] + er[1, s] for s in range(SPECIES)])
        for i in range(4):
            pl.when(ec_from[i])(lambda: ec_copy(i).wait_recv())
        filler = jnp.zeros((N - 16, N), f32)
        side = jnp.concatenate([ec[0] + ec[1], filler], axis=0).T
        corner = jnp.concatenate([ec[2] + ec[3], filler], axis=0).T[N - 8 :]
        side = jnp.concatenate([corner, side], axis=0)
        side = rate_of(*[pltpu.roll(side, N - 3 - 3 * s, 1) for s in range(SPECIES)])
        for s in range(SPECIES):
            e_copy(s).wait_recv()
        middle = rate_of(*[e_own[s] + e_oth[s] for s in range(SPECIES)])
        lane_d = lax.broadcasted_iota(jnp.int32, (N + 8, N), 1)
        rate = [
            jnp.concatenate([edge, middle], axis=0),
            jnp.where(lane_d >= N - 3, side, 0.0),
        ]
        dose = [co[0, i] * rate[i] for i in range(2)]
        for step in range(1, 4):
            ra, rb = pltpu.roll(dose[0], 1, 1), pltpu.roll(dose[1], 1, 1)
            left = (jnp.where(lane_d == 0, rb, ra), jnp.where(lane_d == 0, ra, rb))
            dose = [
                c0[step, i] * dose[i] + cx[step, i] * pltpu.roll(dose[i], 1, 0)
                + cy[step, i] * left[i] + co[step, i] * rate[i]
                for i in range(2)
            ]
        out_f[...] = dose[0][8:]

        for d in range(2):
            @pl.when(x_has[d])
            def _():
                for step in range(2):
                    for c in x_copies(step, d):
                        c.wait_send()
                m_copy(d).wait_send()

            @pl.when(y_has[d])
            def _():
                for step in range(2):
                    y_copy(step, d).wait_send()

        for s in range(SPECIES):
            z_copy(0, s).wait_send()
            z_copy(1, s).wait_send()
            e_copy(s).wait_send()

        @pl.when(has_xn)
        def _():
            for s in range(SPECIES):
                er_copy(s, 0).wait_send()
                er_copy(s, 1).wait_send()

        for i in range(4):
            pl.when(ec_to[i])(lambda: ec_copy(i).wait_send())

    return kernel


def solution(mesh):
    sizes = tuple(mesh.shape[name] for name in ("gx", "gy", "gz"))

    def on_device(tracers, wind_field, band_layer, wall_mask, exit_mask, occupant_count):
        floor = jax.ShapeDtypeStruct((N, N), f32)
        hbm = pl.BlockSpec(memory_space=pl.ANY)
        vmem = pl.BlockSpec(memory_space=pltpu.VMEM)
        V = pltpu.VMEM
        D = pltpu.SemaphoreType.DMA
        return pl.pallas_call(
            make_kernel(sizes),
            out_shape=(jax.ShapeDtypeStruct((SPECIES, L, N, N), f32), floor, floor),
            in_specs=[hbm] * 6,
            out_specs=(vmem, vmem, vmem),
            scratch_shapes=[
                V((SPECIES, L + 2, N + 16, N), f32),
                V((SPECIES, L + 2, N + 16, N), f32),
                V((3, L, N, N), f32),
                V((N, N), jnp.int32),
                V((3, N, N), jnp.int32),
                V((N, N), f32), V((N, N), f32),
                V((2, 72, N), f32), V((2, 2, 72, N), f32),
                V((3, 2, N + 16, N), f32),
                V((4, 2, N + 8, N), f32), V((4, 2, N + 8, N), f32),
                V((4, 2, N + 8, N), f32), V((4, 2, N + 8, N), f32),
                V((SPECIES, N, N), f32), V((SPECIES, N, N), f32),
                V((2, SPECIES, 8, N), f32),
                V((16, N), f32), V((4, 16, N), f32),
                D((L,)), D((L,)), D, D((3,)),
                D((2, SPECIES)), D((2, SPECIES)),
                D((2, 2, L)), D((2, 2, L)), D((2, 2)), D((2, 2)), D((2,)), D((2,)),
                D((SPECIES,)), D((SPECIES,)), D((2, SPECIES)), D((2, SPECIES)),
                D((4,)), D((4,)),
            ],
            compiler_params=pltpu.CompilerParams(
                collective_id=0, has_side_effects=True, vmem_limit_bytes=48 * 1024 * 1024
            ),
        )(*[pltpu.with_memory_space_constraint(a, pltpu.HBM) for a in (tracers, wind_field, band_layer, wall_mask, exit_mask, occupant_count)])

    return jax.shard_map(
        on_device,
        mesh=mesh,
        in_specs=(
            P(None, "gz", "gx", "gy"),
            P(None, "gz", "gx", "gy"),
            P("gx", "gy"),
            P("gx", "gy"),
            P("gx", "gy"),
            P("gx", "gy"),
        ),
        out_specs=(P(None, "gz", "gx", "gy"), P("gx", "gy"), P("gx", "gy")),
        check_vma=False,
    )
```

time: 51 us -> 36.7 us (0.72)
  Pallas kernels: 41.9 us -> 33.6 us
  local copies, waits for them, and re-layouts: 8.11 us -> 2.32 us
    pallas_call x1, Pallas kernels: 41.9 us -> 33.6 us  [on_device(): pl.pallas_call(make_kernel(sizes), out_shape=(jax.ShapeDtypeStruct((SPECI...]
    unnamed x15 -> x3, local copies, waits for them, and re-layouts: 8.11 us -> 2.32 us
where the time goes in v2:
time: 36.7 us; the launch traced here: 36.5 us
  Pallas kernels  33.6 us (92%)
  local copies, waits for them, and re-layouts  2.32 us (6%)
  between operations  0.64 us (2%)
    pallas_call x1, Pallas kernels, on_device(): pl.pallas_call(make_kernel(sizes), out_shape=(jax.ShapeDtypeStruct((SPECI...  33.6 us
    unnamed x3, local copies, waits for them, and re-layouts  2.32 us

profile of v2, /device:TPU:1, one launch (start us, length us, event | category | flops | bytes accessed | tf_op | source)
XLA Modules:
  0.0 36.5 jit_solution(8191497355090253352)
XLA Ops:
  0.6 33.6 %shard_map.85 = (f32[5,4,128,128]{3,2,1,0:T(8,128)S(1)}, f32[128,128]{1,0:T(8,128)S(1)}, f32[128,128]{1,0:T(8,128)S(1)}) custom-call(f32[5,4,128,128]{3,2,1,0:T(8,128)} %tracers.1, f32[3,4,128,128]{3,2,1,0:T(8,128)} %wind.1, s32[128,128]{1,0:T(8,128)} %band_in.1, s32[128,128]{1,0:T(8,128)} %wall_in.1, s32[128,128]{1,0:T(8,128)} %exit_in.1, s32[128,128]{1,0:T(8,128)} %count_in.1), custom_call_target="tpu_custom_call" | custom-call | tf_op jit(solution)/shard_map/pallas_call | solution.py:494
  34.2 1.1 %copy.12 = f32[5,4,128,128]{3,2,1,0:T(8,128)} copy(f32[5,4,128,128]{3,2,1,0:T(8,128)S(1)} %get-tuple-element.6) | data formatting | bytes 2621440
  35.3 0.6 %copy.13 = f32[128,128]{1,0:T(8,128)} copy(f32[128,128]{1,0:T(8,128)S(1)} %get-tuple-element.7) | data formatting | bytes 131072
  35.9 0.6 %copy.14 = f32[128,128]{1,0:T(8,128)} copy(f32[128,128]{1,0:T(8,128)S(1)} %get-tuple-element.8) | data formatting | bytes 131072

commit v3 on v2

--- a/solution.py
+++ b/solution.py
@@ -11,6 +11,8 @@
 N = 128
 CHUNK = 32
 HOLD = 3
+PARTS = ((0, 3), (3, 2))
+EDGE_ROWS = ((0, 72), (0, 32), (24, 24))
 MESH = pl.DeviceIdType.MESH
 f32 = jnp.float32
 
@@ -27,10 +29,10 @@
 
     def kernel(
         tracers, wind, band_in, wall_in, exit_in, count_in,
-        out_t, out_o, out_f,
+        out_t, out_o, c0, cx, cy, co, out_rate,
         t0, t1, wv, band, floor,
         yedge, ypack, ys, yr,
-        m, c0, cx, cy, co,
+        m,
         e_own, e_oth, er, es, ec,
         sem_t, sem_w, sem_b, sem_f,
         z_s, z_r, x_s, x_r, y_s, y_r, m_s, m_r,
@@ -113,15 +115,15 @@
 
         @pl.when(jnp.logical_not(has_yp))
         def _():
-            yr[0, 0] = jnp.zeros((72, N), f32)
-            yr[1, 0] = jnp.zeros((72, N), f32)
+            for step in range(3):
+                yr[step, 0] = jnp.zeros((72, N), f32)
             ec[0] = jnp.zeros((16, N), f32)
             ec[1] = jnp.zeros((16, N), f32)
 
         @pl.when(jnp.logical_not(has_yn))
         def _():
-            yr[0, 1] = jnp.zeros((72, N), f32)
-            yr[1, 1] = jnp.zeros((72, N), f32)
+            for step in range(3):
+                yr[step, 1] = jnp.zeros((72, N), f32)
 
         @pl.when(jnp.logical_not(has_xp & has_yp))
         def _():
@@ -146,12 +148,13 @@
         def x_copies(step, d):
             dev = ((gxn if d == 0 else gxp), gy, gz)
             src, dst = ((N + 7, 7), (8, N + 8))[d]
-            if step == 1:
+            if step > 0:
+                first, count = PARTS[step - 1]
                 return [
                     pltpu.make_async_remote_copy(
-                        t1.at[:, pl.ds(1, L), pl.ds(src, 1), :],
-                        t1.at[:, pl.ds(1, L), pl.ds(dst, 1), :],
-                        x_s.at[1, d, 0], x_r.at[1, d, 0],
+                        t1.at[pl.ds(first, count), pl.ds(1, L), pl.ds(src, 1), :],
+                        t1.at[pl.ds(first, count), pl.ds(1, L), pl.ds(dst, 1), :],
+                        x_s.at[step, d, 0], x_r.at[step, d, 0],
                         device_id=dev, device_id_type=MESH,
                     )
                 ]
@@ -166,9 +169,9 @@
             ]
 
         def y_copy(step, d):
-            rows = 72 if step == 0 else 48
+            first, rows = EDGE_ROWS[step]
             return pltpu.make_async_remote_copy(
-                ys.at[step, pl.ds(0, rows), :], yr.at[step, d, pl.ds(0, rows), :],
+                ys.at[step, pl.ds(first, rows), :], yr.at[step, d, pl.ds(first, rows), :],
                 y_s.at[step, d], y_r.at[step, d],
                 device_id=(gx, (gyn if d == 0 else gyp), gz), device_id_type=MESH,
             )
@@ -314,18 +317,20 @@
                 for r in chunks:
                     t1[s, l + 1, pl.ds(8 + r, CHUNK), :] = moved(t0, s, l, r, k)
 
-            @pl.when(s < 2)
+            @pl.when(s != 2)
             def _():
                 z_copy(1, s).start()
 
             pack_y(t1, s)
             return carry
 
-        lax.fori_loop(0, SPECIES, first, 0)
+        lax.fori_loop(0, 3, first, 0)
         send_x(1)
         send_y(1)
-        for s in range(2, SPECIES):
-            z_copy(1, s).start()
+        z_copy(1, 2).start()
+        lax.fori_loop(3, SPECIES, first, 0)
+        send_x(2)
+        send_y(2)
 
         for d in range(2):
             pl.when(x_has[1 - d])(lambda: m_copy(d).wait_recv())
@@ -400,7 +405,11 @@
 
             return carry
 
-        lax.fori_loop(0, SPECIES, second, 0)
+        lax.fori_loop(0, 3, second, 0)
+        recv_x(2)
+        recv_y(2)
+        unpack_y(2)
+        lax.fori_loop(3, SPECIES, second, 0)
         strip = jnp.zeros((N, N), f32)
         for s in range(SPECIES):
             mine = (wide >= 3 * s) & (wide < 3 * s + 3)
@@ -437,32 +446,21 @@
             e_copy(s).wait_recv()
         middle = rate_of(*[e_own[s] + e_oth[s] for s in range(SPECIES)])
         lane_d = lax.broadcasted_iota(jnp.int32, (N + 8, N), 1)
-        rate = [
-            jnp.concatenate([edge, middle], axis=0),
-            jnp.where(lane_d >= N - 3, side, 0.0),
-        ]
-        dose = [co[0, i] * rate[i] for i in range(2)]
-        for step in range(1, 4):
-            ra, rb = pltpu.roll(dose[0], 1, 1), pltpu.roll(dose[1], 1, 1)
-            left = (jnp.where(lane_d == 0, rb, ra), jnp.where(lane_d == 0, ra, rb))
-            dose = [
-                c0[step, i] * dose[i] + cx[step, i] * pltpu.roll(dose[i], 1, 0)
-                + cy[step, i] * left[i] + co[step, i] * rate[i]
-                for i in range(2)
-            ]
-        out_f[...] = dose[0][8:]
+        out_rate[0, pl.ds(0, 8), :] = edge
+        out_rate[0, pl.ds(8, N), :] = middle
+        out_rate[1] = jnp.where(lane_d >= N - 3, side, 0.0)
 
         for d in range(2):
             @pl.when(x_has[d])
             def _():
-                for step in range(2):
+                for step in range(3):
                     for c in x_copies(step, d):
                         c.wait_send()
                 m_copy(d).wait_send()
 
             @pl.when(y_has[d])
             def _():
-                for step in range(2):
+                for step in range(3):
                     y_copy(step, d).wait_send()
 
         for s in range(SPECIES):
@@ -482,20 +480,49 @@
     return kernel
 
 
+def finish(fields, occupants, c0, cx, cy, co, rate, out_t, out_o, out_f, dose_v, sem_t, sem_o, sem_f):
+    copies = [
+        pltpu.make_async_copy(fields.at[s], out_t.at[s], sem_t.at[s]) for s in range(SPECIES)
+    ]
+    copies.append(pltpu.make_async_copy(occupants, out_o, sem_o))
+    for c in copies:
+        c.start()
+    lane = lax.broadcasted_iota(jnp.int32, (N + 8, N), 1)
+    dose = [co[0, i] * rate[i] for i in range(2)]
+    for step in range(1, 4):
+        ra, rb = pltpu.roll(dose[0], 1, 1), pltpu.roll(dose[1], 1, 1)
+        left = (jnp.where(lane == 0, rb, ra), jnp.where(lane == 0, ra, rb))
+        dose = [
+            c0[step, i] * dose[i] + cx[step, i] * pltpu.roll(dose[i], 1, 0)
+            + cy[step, i] * left[i] + co[step, i] * rate[i]
+            for i in range(2)
+        ]
+    dose_v[...] = dose[0][8:]
+    copies.append(pltpu.make_async_copy(dose_v, out_f, sem_f))
+    copies[-1].start()
+    for c in copies:
+        c.wait()
+
+
 def solution(mesh):
     sizes = tuple(mesh.shape[name] for name in ("gx", "gy", "gz"))
 
     def on_device(tracers, wind_field, band_layer, wall_mask, exit_mask, occupant_count):
         floor = jax.ShapeDtypeStruct((N, N), f32)
-        hbm = pl.BlockSpec(memory_space=pl.ANY)
+        hbm = pl.BlockSpec(memory_space=pltpu.HBM)
         vmem = pl.BlockSpec(memory_space=pltpu.VMEM)
         V = pltpu.VMEM
         D = pltpu.SemaphoreType.DMA
-        return pl.pallas_call(
+        weights = jax.ShapeDtypeStruct((4, 2, N + 8, N), f32)
+        cells = jax.ShapeDtypeStruct((SPECIES, L, N, N), f32)
+        found = pl.pallas_call(
             make_kernel(sizes),
-            out_shape=(jax.ShapeDtypeStruct((SPECIES, L, N, N), f32), floor, floor),
+            out_shape=(
+                cells, floor, weights, weights, weights, weights,
+                jax.ShapeDtypeStruct((2, N + 8, N), f32),
+            ),
             in_specs=[hbm] * 6,
-            out_specs=(vmem, vmem, vmem),
+            out_specs=(vmem,) * 7,
             scratch_shapes=[
                 V((SPECIES, L + 2, N + 16, N), f32),
                 V((SPECIES, L + 2, N + 16, N), f32),
@@ -503,23 +530,29 @@
                 V((N, N), jnp.int32),
                 V((3, N, N), jnp.int32),
                 V((N, N), f32), V((N, N), f32),
-                V((2, 72, N), f32), V((2, 2, 72, N), f32),
+                V((3, 72, N), f32), V((3, 2, 72, N), f32),
                 V((3, 2, N + 16, N), f32),
-                V((4, 2, N + 8, N), f32), V((4, 2, N + 8, N), f32),
-                V((4, 2, N + 8, N), f32), V((4, 2, N + 8, N), f32),
                 V((SPECIES, N, N), f32), V((SPECIES, N, N), f32),
                 V((2, SPECIES, 8, N), f32),
                 V((16, N), f32), V((4, 16, N), f32),
                 D((L,)), D((L,)), D, D((3,)),
                 D((2, SPECIES)), D((2, SPECIES)),
-                D((2, 2, L)), D((2, 2, L)), D((2, 2)), D((2, 2)), D((2,)), D((2,)),
+                D((3, 2, L)), D((3, 2, L)), D((3, 2)), D((3, 2)), D((2,)), D((2,)),
                 D((SPECIES,)), D((SPECIES,)), D((2, SPECIES)), D((2, SPECIES)),
                 D((4,)), D((4,)),
             ],
             compiler_params=pltpu.CompilerParams(
-                collective_id=0, has_side_effects=True, vmem_limit_bytes=48 * 1024 * 1024
+                collective_id=0, has_side_effects=True, vmem_limit_bytes=32 * 1024 * 1024
             ),
         )(*[pltpu.with_memory_space_constraint(a, pltpu.HBM) for a in (tracers, wind_field, band_layer, wall_mask, exit_mask, occupant_count)])
+        return pl.pallas_call(
+            finish,
+            out_shape=(cells, floor, floor),
+            in_specs=[vmem] * 7,
+            out_specs=(hbm,) * 3,
+            scratch_shapes=[V((N, N), f32), D((SPECIES,)), D, D],
+            compiler_params=pltpu.CompilerParams(vmem_limit_bytes=16 * 1024 * 1024),
+        )(*found)
 
     return jax.shard_map(
         on_device,

time: 36.7 us -> 35.2 us (0.959)
  the two profiles are of different devices: /device:TPU:1 before, /device:TPU:211 now
where the time goes in v3:
time: 35.2 us; the launch traced here: 35 us
  Pallas kernels  34.4 us (98%)
  between operations  0.64 us (2%)
    pallas_call x1, Pallas kernels, on_device(): pl.pallas_call(make_kernel(sizes), out_shape=(cells, floor, weights, weig...  33 us
    pallas_call x1, Pallas kernels, on_device(): pl.pallas_call(finish, out_shape=(cells, floor, floor), in_specs=[vmem] *...  1.36 us

profile of v3, /device:TPU:211, one launch (start us, length us, event | category | flops | bytes accessed | tf_op | source)
XLA Modules:
  0.0 35.0 jit_solution(9109057736041283964)
XLA Ops:
  0.6 33.0 %shard_map.85 = (f32[5,4,128,128]{3,2,1,0:T(8,128)S(1)}, f32[128,128]{1,0:T(8,128)S(1)}, f32[4,2,136,128]{3,2,1,0:T(8,128)S(1)}, f32[4,2,136,128]{3,2,1,0:T(8,12...) custom-call(f32[5,4,128,128]{3,2,1,0:T(8,128)} %tracers.1, ...), custom_call_target="tpu_custom_call" | custom-call | tf_op jit(solution)/shard_map/pallas_call | solution.py:518
  33.7 1.4 %shard_map.86 = (f32[5,4,128,128]{3,2,1,0:T(8,128)}, f32[128,128]{1,0:T(8,128)}, f32[128,128]{1,0:T(8,128)}) custom-call(f32[5,4,128,128]{3,2,1,0:T(8,128)S(1)} %get-tuple-element.10.fields, f32[128,128]{1,0:T(8,128)S(1)} %get-tuple-element.11.occupants, f32[4,2,136,128]{3,2,1,0:T(8,128)S(1)} %get-tuple-element.12.c0, ...), custom_call_target="tpu_custom_call" | custom-call | tf_op jit(solution)/shard_map/pallas_call | solution.py:548

commit v4 on v3

--- a/solution.py
+++ b/solution.py
@@ -11,6 +11,7 @@
 N = 128
 CHUNK = 32
 HOLD = 3
+BEFORE = 4
 PARTS = ((0, 3), (3, 2))
 EDGE_ROWS = ((0, 72), (0, 32), (24, 24))
 MESH = pl.DeviceIdType.MESH
@@ -36,7 +37,7 @@
         e_own, e_oth, er, es, ec,
         sem_t, sem_w, sem_b, sem_f,
         z_s, z_r, x_s, x_r, y_s, y_r, m_s, m_r,
-        e_s, e_r, er_s, er_r, ec_s, ec_r,
+        e_s, e_r, er_s, er_r, ec_s, ec_r, here_x, here_y,
     ):
         gx, gy, gz = lax.axis_index("gx"), lax.axis_index("gy"), lax.axis_index("gz")
         oz = 1 - gz
@@ -79,11 +80,14 @@
                 pl.semaphore_signal(barrier, inc=1, device_id=dev, device_id_type=MESH)
 
         greet((gx, gy, oz))
-        pl.when(has_xn)(lambda: greet((gxn, gy, gz)))
-        pl.when(has_xp)(lambda: greet((gxp, gy, gz), (gxp, gy, oz)))
-        pl.when(has_yn)(lambda: greet((gx, gyn, gz)))
-        pl.when(has_yp)(lambda: greet((gx, gyp, gz), (gx, gyp, oz)))
-        pl.when(has_xp & has_yp)(lambda: greet((gxp, gyp, gz), (gxp, gyp, oz)))
+        odd_y, even_y = lax.rem(gy, 2) == 1, lax.rem(gy, 2) == 0
+        speaks_x = ((gx > 0) & has_xn, gx == 1)
+        waits_x = ((gx == 0) & has_xn, gx > 1)
+        x_dev = ((gxn, gy, gz), (gxp, gy, gz))
+        y_dev = ((gx, gyn, gz), (gx, gyp, gz))
+        for d in range(2):
+            pl.when(speaks_x[d])(lambda: greet(x_dev[d]))
+            pl.when(odd_y & y_has[d])(lambda: greet(y_dev[d]))
 
         def clear(s, carry):
             t0[s, 0, pl.ds(8, N), :] = jnp.zeros((N, N), f32)
@@ -133,9 +137,16 @@
         one = lambda flag: flag.astype(jnp.int32)
         pl.semaphore_wait(
             barrier,
-            1 + 2 * one(has_xn) + one(has_xp) + 2 * one(has_yn) + one(has_yp)
-            + 2 * one(has_xn) * one(has_yn),
+            1 + one(waits_x[0]) + one(waits_x[1])
+            + one(even_y) * (one(has_yn) + one(has_yp)),
         )
+
+        def answer(sem, dev):
+            pl.semaphore_signal(sem, inc=1, device_id=dev, device_id_type=MESH)
+
+        for d in range(2):
+            pl.when(waits_x[d])(lambda: answer(here_x.at[1 - d], x_dev[d]))
+            pl.when(even_y & y_has[d])(lambda: answer(here_y.at[1 - d], y_dev[d]))
 
         def z_copy(step, s):
             src = tracers.at[s, boundary] if step == 0 else t1.at[s, L, pl.ds(8, N), :]
@@ -184,9 +195,9 @@
                 device_id=((gxn if d == 0 else gxp), gy, gz), device_id_type=MESH,
             )
 
-        def send_x(step):
+        def send_x(step, when=x_has):
             for d in range(2):
-                @pl.when(x_has[d])
+                @pl.when(when[d])
                 def _():
                     for c in x_copies(step, d):
                         c.start()
@@ -216,12 +227,13 @@
             )
 
         def ec_copy(i):
-            dev = ((gx, gyn, gz), (gx, gyn, oz), (gxn, gyn, gz), (gxn, gyn, oz))[i]
+            dev = ((gx, gyn, gz), (gx, gyn, oz), (gxn, gyn, gz), (gx, gy, oz))[i]
             return pltpu.make_async_remote_copy(
-                es, ec.at[i], ec_s.at[i], ec_r.at[i], device_id=dev, device_id_type=MESH
-            )
-
-        send_x(0)
+                (ec.at[2] if i == 3 else es), ec.at[i], ec_s.at[i], ec_r.at[i],
+                device_id=dev, device_id_type=MESH,
+            )
+
+        send_x(0, waits_x)
         z_copy(0, 0).start()
         z_copy(0, 1).start()
 
@@ -294,8 +306,16 @@
             return carry
 
         lax.fori_loop(0, SPECIES, pack_y0, 0)
+        for s in range(2, BEFORE):
+            z_copy(0, s).start()
+
+        for d in range(2):
+            pl.when(speaks_x[d])(lambda: pl.semaphore_wait(here_x.at[d], 1))
+        send_x(0, speaks_x)
+        for d in range(2):
+            pl.when(odd_y & y_has[d])(lambda: pl.semaphore_wait(here_y.at[d], 1))
         send_y(0)
-        for s in range(2, SPECIES):
+        for s in range(BEFORE, SPECIES):
             z_copy(0, s).start()
         for c in loads_w:
             c.wait()
@@ -415,9 +435,9 @@
             mine = (wide >= 3 * s) & (wide < 3 * s + 3)
             strip = jnp.where(mine, pltpu.roll(e_own[s], 3 * s + 3, 1), strip)
         es[...] = strip.T[:16]
-        ec_to = (has_yn, has_yn, has_xn & has_yn, has_xn & has_yn)
+        ec_to = (has_yn, has_yn, has_xn & has_yn, has_xp & has_yp)
         ec_from = (has_yp, has_yp, has_xp & has_yp, has_xp & has_yp)
-        for i in range(4):
+        for i in range(3):
             pl.when(ec_to[i])(lambda: ec_copy(i).start())
         for s in range(HOLD, SPECIES):
             e_copy(s).start()
@@ -435,8 +455,10 @@
                 er_copy(s, 1).wait_recv()
 
         edge = rate_of(*[er[0, s] + er[1, s] for s in range(SPECIES)])
-        for i in range(4):
+        for i in range(3):
             pl.when(ec_from[i])(lambda: ec_copy(i).wait_recv())
+        pl.when(ec_from[3])(lambda: ec_copy(3).start())
+        pl.when(ec_from[3])(lambda: ec_copy(3).wait_recv())
         filler = jnp.zeros((N - 16, N), f32)
         side = jnp.concatenate([ec[0] + ec[1], filler], axis=0).T
         corner = jnp.concatenate([ec[2] + ec[3], filler], axis=0).T[N - 8 :]
@@ -513,6 +535,7 @@
         vmem = pl.BlockSpec(memory_space=pltpu.VMEM)
         V = pltpu.VMEM
         D = pltpu.SemaphoreType.DMA
+        R = pltpu.SemaphoreType.REGULAR
         weights = jax.ShapeDtypeStruct((4, 2, N + 8, N), f32)
         cells = jax.ShapeDtypeStruct((SPECIES, L, N, N), f32)
         found = pl.pallas_call(
@@ -540,6 +563,7 @@
                 D((3, 2, L)), D((3, 2, L)), D((3, 2)), D((3, 2)), D((2,)), D((2,)),
                 D((SPECIES,)), D((SPECIES,)), D((2, SPECIES)), D((2, SPECIES)),
                 D((4,)), D((4,)),
+                R((2,)), R((2,)),
             ],
             compiler_params=pltpu.CompilerParams(
                 collective_id=0, has_side_effects=True, vmem_limit_bytes=32 * 1024 * 1024

time: 35.2 us -> 34.8 us (0.989)
  the two profiles are of different devices: /device:TPU:211 before, /device:TPU:65 now
where the time goes in v4:
time: 34.8 us; the launch traced here: 34.6 us
  Pallas kernels  34 us (98%)
  between operations  0.64 us (2%)
    pallas_call x1, Pallas kernels, on_device(): pl.pallas_call(make_kernel(sizes), out_shape=(cells, floor, weights, weig...  32.6 us
    pallas_call x1, Pallas kernels, on_device(): pl.pallas_call(finish, out_shape=(cells, floor, floor), in_specs=[vmem] *...  1.36 us

profile of v4, /device:TPU:65, one launch (start us, length us, event | category | flops | bytes accessed | tf_op | source)
XLA Modules:
  0.0 34.6 jit_solution(2959629445310577957)
XLA Ops:
  0.6 32.6 %shard_map.85 = (f32[5,4,128,128]{3,2,1,0:T(8,128)S(1)}, f32[128,128]{1,0:T(8,128)S(1)}, f32[4,2,136,128]{3,2,1,0:T(8,128)S(1)}, f32[4,2,136,128]{3,2,1,0:T(8,12...) custom-call(f32[5,4,128,128]{3,2,1,0:T(8,128)} %tracers.1, ...), custom_call_target="tpu_custom_call" | custom-call | tf_op jit(solution)/shard_map/pallas_call | solution.py:541
  33.3 1.4 %shard_map.86 = (f32[5,4,128,128]{3,2,1,0:T(8,128)}, f32[128,128]{1,0:T(8,128)}, f32[128,128]{1,0:T(8,128)}) custom-call(f32[5,4,128,128]{3,2,1,0:T(8,128)S(1)} %get-tuple-element.10.fields, f32[128,128]{1,0:T(8,128)S(1)} %get-tuple-element.11.occupants, f32[4,2,136,128]{3,2,1,0:T(8,128)S(1)} %get-tuple-element.12.c0, ...), custom_call_target="tpu_custom_call" | custom-call | tf_op jit(solution)/shard_map/pallas_call | solution.py:572

commit v5 on v4

--- a/solution.py
+++ b/solution.py
@@ -1,3 +1,5 @@
+import functools
+
 import jax
 import jax.numpy as jnp
 from jax import lax
@@ -32,7 +34,7 @@
         tracers, wind, band_in, wall_in, exit_in, count_in,
         out_t, out_o, c0, cx, cy, co, out_rate,
         t0, t1, wv, band, floor,
-        yedge, ypack, ys, yr,
+        yedge, ypack, ys, yr, xs, xr,
         m,
         e_own, e_oth, er, es, ec,
         sem_t, sem_w, sem_b, sem_f,
@@ -160,11 +162,11 @@
             dev = ((gxn if d == 0 else gxp), gy, gz)
             src, dst = ((N + 7, 7), (8, N + 8))[d]
             if step > 0:
-                first, count = PARTS[step - 1]
+                rows = L * PARTS[step - 1][1]
                 return [
                     pltpu.make_async_remote_copy(
-                        t1.at[pl.ds(first, count), pl.ds(1, L), pl.ds(src, 1), :],
-                        t1.at[pl.ds(first, count), pl.ds(1, L), pl.ds(dst, 1), :],
+                        xs.at[step - 1, d, pl.ds(0, rows), :],
+                        xr.at[step - 1, d, pl.ds(0, rows), :],
                         x_s.at[step, d, 0], x_r.at[step, d, 0],
                         device_id=dev, device_id_type=MESH,
                     )
@@ -233,8 +235,8 @@
                 device_id=dev, device_id_type=MESH,
             )
 
+        z_copy(0, 0).start()
         send_x(0, waits_x)
-        z_copy(0, 0).start()
         z_copy(0, 1).start()
 
         lane = lax.broadcasted_iota(jnp.int32, (CHUNK, N), 1)
@@ -330,7 +332,15 @@
             pl.when(x_has[d])(lambda: m_copy(d).start())
         recv_x(0)
 
-        def first(s, carry):
+        def unpack_x(part):
+            first, count = PARTS[part]
+            for d, row in enumerate((7, N + 8)):
+                @pl.when(x_has[1 - d])
+                def _():
+                    for j in range(L * count):
+                        t1[first + j // L, 1 + j % L, pl.ds(row, 1), :] = xr[part, d, pl.ds(j, 1), :]
+
+        def first(part, s, carry):
             k = coefficient_of(s)
             z_copy(0, s).wait_recv()
             for l in (L - 1, 0, 1, 2):
@@ -342,13 +352,17 @@
                 z_copy(1, s).start()
 
             pack_y(t1, s)
+            for l in range(L):
+                j = (s - PARTS[part][0]) * L + l
+                xs[part, 0, pl.ds(j, 1), :] = t1[s, l + 1, pl.ds(N + 7, 1), :]
+                xs[part, 1, pl.ds(j, 1), :] = t1[s, l + 1, pl.ds(8, 1), :]
             return carry
 
-        lax.fori_loop(0, 3, first, 0)
+        lax.fori_loop(0, 3, functools.partial(first, 0), 0)
         send_x(1)
         send_y(1)
         z_copy(1, 2).start()
-        lax.fori_loop(3, SPECIES, first, 0)
+        lax.fori_loop(3, SPECIES, functools.partial(first, 1), 0)
         send_x(2)
         send_y(2)
 
@@ -391,6 +405,7 @@
         out_o[...] = occ[0][8 : N + 8]
 
         recv_x(1)
+        unpack_x(0)
         recv_y(1)
         unpack_y(1)
 
@@ -427,6 +442,7 @@
 
         lax.fori_loop(0, 3, second, 0)
         recv_x(2)
+        unpack_x(1)
         recv_y(2)
         unpack_y(2)
         lax.fori_loop(3, SPECIES, second, 0)
@@ -554,6 +570,7 @@
                 V((3, N, N), jnp.int32),
                 V((N, N), f32), V((N, N), f32),
                 V((3, 72, N), f32), V((3, 2, 72, N), f32),
+                V((2, 2, 16, N), f32), V((2, 2, 16, N), f32),
                 V((3, 2, N + 16, N), f32),
                 V((SPECIES, N, N), f32), V((SPECIES, N, N), f32),
                 V((2, SPECIES, 8, N), f32),

time: 34.8 us -> 34.8 us (level)
  no operation moved by 1% of the time
where the time goes in v5:
time: 34.8 us; the launch traced here: 34.6 us
  Pallas kernels  34 us (98%)
  between operations  0.64 us (2%)
    pallas_call x1, Pallas kernels, on_device(): pl.pallas_call(make_kernel(sizes), out_shape=(cells, floor, weights, weig...  32.6 us
    pallas_call x1, Pallas kernels, on_device(): pl.pallas_call(finish, out_shape=(cells, floor, floor), in_specs=[vmem] *...  1.36 us

profile of v5, /device:TPU:65, one launch (start us, length us, event | category | flops | bytes accessed | tf_op | source)
XLA Modules:
  0.0 34.6 jit_solution(7828094316325419893)
XLA Ops:
  0.6 32.6 %shard_map.85 = (f32[5,4,128,128]{3,2,1,0:T(8,128)S(1)}, f32[128,128]{1,0:T(8,128)S(1)}, f32[4,2,136,128]{3,2,1,0:T(8,128)S(1)}, f32[4,2,136,128]{3,2,1,0:T(8,12...) custom-call(f32[5,4,128,128]{3,2,1,0:T(8,128)} %tracers.1, ...), custom_call_target="tpu_custom_call" | custom-call | tf_op jit(solution)/shard_map/pallas_call | solution.py:557
  33.3 1.4 %shard_map.86 = (f32[5,4,128,128]{3,2,1,0:T(8,128)}, f32[128,128]{1,0:T(8,128)}, f32[128,128]{1,0:T(8,128)}) custom-call(f32[5,4,128,128]{3,2,1,0:T(8,128)S(1)} %get-tuple-element.10.fields, f32[128,128]{1,0:T(8,128)S(1)} %get-tuple-element.11.occupants, f32[4,2,136,128]{3,2,1,0:T(8,128)S(1)} %get-tuple-element.12.c0, ...), custom_call_target="tpu_custom_call" | custom-call | tf_op jit(solution)/shard_map/pallas_call | solution.py:589

commit v6 on v5

--- a/solution.py
+++ b/solution.py
@@ -34,7 +34,7 @@
         tracers, wind, band_in, wall_in, exit_in, count_in,
         out_t, out_o, c0, cx, cy, co, out_rate,
         t0, t1, wv, band, floor,
-        yedge, ypack, ys, yr, xs, xr,
+        yedge, ypack, middle, ys, yr, xs, xr,
         m,
         e_own, e_oth, er, es, ec,
         sem_t, sem_w, sem_b, sem_f,
@@ -480,13 +480,16 @@
         corner = jnp.concatenate([ec[2] + ec[3], filler], axis=0).T[N - 8 :]
         side = jnp.concatenate([corner, side], axis=0)
         side = rate_of(*[pltpu.roll(side, N - 3 - 3 * s, 1) for s in range(SPECIES)])
-        for s in range(SPECIES):
+        out_rate[0, pl.ds(0, 8), :] = edge
+        for s in range(SPECIES - 1):
             e_copy(s).wait_recv()
-        middle = rate_of(*[e_own[s] + e_oth[s] for s in range(SPECIES)])
         lane_d = lax.broadcasted_iota(jnp.int32, (N + 8, N), 1)
-        out_rate[0, pl.ds(0, 8), :] = edge
-        out_rate[0, pl.ds(8, N), :] = middle
         out_rate[1] = jnp.where(lane_d >= N - 3, side, 0.0)
+        zero = jnp.zeros((N, N), f32)
+        middle[...] = rate_of(*[e_own[s] + e_oth[s] for s in range(SPECIES - 1)], zero)
+        e_copy(SPECIES - 1).wait_recv()
+        heat = e_own[SPECIES - 1] + e_oth[SPECIES - 1]
+        out_rate[0, pl.ds(8, N), :] = middle[...] + 0.1 * heat * heat
 
         for d in range(2):
             @pl.when(x_has[d])
@@ -568,7 +571,7 @@
                 V((3, L, N, N), f32),
                 V((N, N), jnp.int32),
                 V((3, N, N), jnp.int32),
-                V((N, N), f32), V((N, N), f32),
+                V((N, N), f32), V((N, N), f32), V((N, N), f32),
                 V((3, 72, N), f32), V((3, 2, 72, N), f32),
                 V((2, 2, 16, N), f32), V((2, 2, 16, N), f32),
                 V((3, 2, N + 16, N), f32),

time: 34.8 us -> 34.8 us (level)
  no operation moved by 1% of the time
where the time goes in v6:
time: 34.8 us; the launch traced here: 34.7 us
  Pallas kernels  34 us (98%)
  between operations  0.64 us (2%)
    pallas_call x1, Pallas kernels, on_device(): pl.pallas_call(make_kernel(sizes), out_shape=(cells, floor, weights, weig...  32.7 us
    pallas_call x1, Pallas kernels, on_device(): pl.pallas_call(finish, out_shape=(cells, floor, floor), in_specs=[vmem] *...  1.36 us

profile of v6, /device:TPU:65, one launch (start us, length us, event | category | flops | bytes accessed | tf_op | source)
XLA Modules:
  0.0 34.7 jit_solution(6925156430401747228)
XLA Ops:
  0.6 32.7 %shard_map.85 = (f32[5,4,128,128]{3,2,1,0:T(8,128)S(1)}, f32[128,128]{1,0:T(8,128)S(1)}, f32[4,2,136,128]{3,2,1,0:T(8,128)S(1)}, f32[4,2,136,128]{3,2,1,0:T(8,12...) custom-call(f32[5,4,128,128]{3,2,1,0:T(8,128)} %tracers.1, ...), custom_call_target="tpu_custom_call" | custom-call | tf_op jit(solution)/shard_map/pallas_call | solution.py:560
  33.3 1.4 %shard_map.86 = (f32[5,4,128,128]{3,2,1,0:T(8,128)}, f32[128,128]{1,0:T(8,128)}, f32[128,128]{1,0:T(8,128)}) custom-call(f32[5,4,128,128]{3,2,1,0:T(8,128)S(1)} %get-tuple-element.10.fields, f32[128,128]{1,0:T(8,128)S(1)} %get-tuple-element.11.occupants, f32[4,2,136,128]{3,2,1,0:T(8,128)S(1)} %get-tuple-element.12.c0, ...), custom_call_target="tpu_custom_call" | custom-call | tf_op jit(solution)/shard_map/pallas_call | solution.py:592
